TPU v7x, 512 devices: a whole 4x4x16 slice. The times are simulated.
512 devices in a mesh: slab: 8 (over x, core), energy: 64 (over z, y).
Axes of the slice: x: 4, y: 4, z: 16, core: 2. Of those that a mesh axis runs over, the one named last changes fastest.
Arguments:
- retarded: bfloat16 [128, 3, 1536, 384], P('energy', None, 'slab'), may hold values from -0.3125 to 0.3125
- injection: bfloat16 [128, 2, 1536, 384], P('energy', None, 'slab'), may hold values from -6 to 6
- screened: bfloat16 [128, 2, 1536, 384], P('energy', None, 'slab'), may hold values from -6 to 6
- pattern: int32 [1536], P('slab'), may hold values from 0 to 1, as said below
Outputs:
- self_energy: bfloat16 [128, 2, 1536, 384], P('energy', None, 'slab')
Inputs may be any that keep to these rules, and one draw needn't show every extreme that they name: `pattern`: exactly 128 of the 192 entries held by each index of slab are 1.
All inputs are finite; a program needn't handle non-finite values.
Results may differ from a plain program's by a relative error of at most 0.0058.
Values may be sent and summed in bfloat16 or wider, within the bound.
No kernel may reach another device: no remote copies, remote signals or barrier semaphores. Data moves between devices by JAX's collectives and lax.ppermute only.
A program may use at most 64 MiB of HBM per device.

v0:
```python
import math

import jax
import jax.numpy as jnp
from jax import lax
from jax.sharding import PartitionSpec as P

B = 192


def with_halo(cells, sides, width):
    for axis, dim in sides:
        count = lax.axis_size(axis)
        ends = count - 1
        head = lax.slice_in_dim(cells, 0, width, axis=dim)
        tail = lax.slice_in_dim(cells, cells.shape[dim] - width, cells.shape[dim], axis=dim)
        cells = jnp.concatenate(
            [
                lax.ppermute(tail, axis, [(i, (i + 1) % count) for i in range(ends)]),
                cells,
                lax.ppermute(head, axis, [((i + 1) % count, i) for i in range(ends)]),
            ],
            axis=dim,
        )
    return cells


def stack_complex(blocks):
    half = blocks.shape[-1] // 2
    real_part = blocks[..., :half]
    imag_part = blocks[..., half:]
    upper = jnp.concatenate([real_part, imag_part], -1)
    lower = jnp.concatenate([-imag_part, real_part], -1)
    return jnp.concatenate([upper, lower], -2)


def split_table(table):
    high_part = lax.optimization_barrier(table.astype(jnp.bfloat16))
    low_part = (table - high_part.astype(jnp.float32)).astype(jnp.bfloat16)
    return (high_part, low_part)


def convolve(green, screen):
    count = green.shape[0]
    half = green.shape[-1] // 2
    energy_index = jnp.arange(count, dtype=jnp.int32)
    phase_angle = (
        2.0
        * math.pi
        / count
        * (energy_index[:, None] * energy_index[None, :] % count).astype(jnp.float32)
    )
    cosine_table = jnp.cos(phase_angle)
    sine_table = jnp.sin(phase_angle)
    cosine_high, cosine_low = split_table(cosine_table)
    sine_high, sine_low = split_table(sine_table)

    def apply_split(high_part, low_part, flat):
        first_pass = jnp.dot(high_part, flat, preferred_element_type=jnp.float32)
        return first_pass + jnp.dot(low_part, flat, preferred_element_type=jnp.float32)

    def forward(values):
        flat = values.reshape(count, -1)
        with_cos = apply_split(cosine_high, cosine_low, flat).reshape(values.shape)
        with_sin = apply_split(sine_high, sine_low, flat).reshape(values.shape)
        return (
            with_cos[..., :half] + with_sin[..., half:],
            with_cos[..., half:] - with_sin[..., :half],
        )

    green_real, green_imag = forward(green)
    screen_real, screen_imag = forward(screen)
    prod_real = green_real * screen_real - green_imag * screen_imag
    prod_imag = green_real * screen_imag + green_imag * screen_real
    values = jnp.concatenate([prod_real, prod_imag], -1)
    flat = values.reshape(count, -1)
    with_cos = jnp.dot(cosine_table, flat, precision=lax.Precision.HIGH).reshape(values.shape)
    with_sin = jnp.dot(sine_table, flat, precision=lax.Precision.HIGH).reshape(values.shape)
    with_cos, with_sin = (with_cos, with_sin)
    sigma_real = with_cos[..., :half] - with_sin[..., half:]
    sigma_imag = with_cos[..., half:] + with_sin[..., :half]
    factor = 1.0 / (count * math.sqrt(count))
    return jnp.concatenate([-sigma_imag, sigma_real], -1) * factor


def local(retarded, injection, screened, pattern):
    energy_count = retarded.shape[0]
    row_count = retarded.shape[2]
    block_count = row_count // B
    padded = with_halo(injection, (("slab", 2),), B)
    padded = padded.reshape(energy_count, 2, block_count + 2, B, 2 * B)
    row_blocks = retarded.reshape(energy_count, 3, block_count, B, 2 * B)
    total = jnp.zeros((energy_count, 2, block_count, B, 2 * B), jnp.float32)
    for offset in range(3):
        nearby = padded[:, :, offset : offset + block_count]
        expanded = stack_complex(nearby)
        row_block = row_blocks[:, offset]
        left_product = jnp.einsum(
            "enac,elncd->elnad", row_block, expanded, preferred_element_type=jnp.float32
        ).astype(jnp.bfloat16)
        swapped = jnp.concatenate([left_product[..., B:], -left_product[..., :B]], -1)
        real_part = jnp.einsum(
            "elnac,enbc->elnab", left_product, row_block, preferred_element_type=jnp.float32
        )
        imag_part = jnp.einsum(
            "elnac,enbc->elnab", swapped, row_block, preferred_element_type=jnp.float32
        )
        total = total + jnp.concatenate([real_part, imag_part], -1)
    green = total.astype(jnp.bfloat16).reshape(energy_count, 2, row_count, 2 * B)
    green_owned, screen_owned = (
        lax.all_to_all(green, "energy", split_axis=2, concat_axis=0, tiled=True),
        lax.all_to_all(screened, "energy", split_axis=2, concat_axis=0, tiled=True),
    )
    sigma = convolve(green_owned, screen_owned).astype(jnp.bfloat16)
    returned_rows = lax.all_to_all(sigma, "energy", split_axis=0, concat_axis=2, tiled=True)
    result = returned_rows * pattern.astype(jnp.bfloat16)[None, None, :, None]
    return result


def solution(mesh):
    placed = (
        P("energy", None, "slab", None),
        P("energy", None, "slab", None),
        P("energy", None, "slab", None),
        P("slab"),
    )
    return jax.shard_map(
        local,
        mesh=mesh,
        in_specs=placed,
        out_specs=P("energy", None, "slab", None),
        check_vma=False,
    )
```

profile of v0, /device:TPU:16, one launch (start us, length us, event | category | flops | bytes accessed | tf_op | source)
XLA Modules:
  0.0 167.6 jit_solution(8449225784450031116)
XLA Ops:
  0.0 1.4 collective-permute-start.1
  1.4 3.1 %collective-permute-start = (bf16[2,2,192,384]{3,2,1,0:T(8,128)(2,1)}, bf16[2,2,192,384]{3,2,1,0:T(8,128)(2,1)S(1)}, u32[]{:S(2)}, u32[]{:S(2)}) collective-permute-start(bf16[2,2,192,384]{3,2,1,0:T(8,128)(2,1)} %param.5), channel_id=1, source_target_pairs={{0,64},{64,128},{128,192},{192,256},{256,320},{320,384},{384,448},... | collective-permute-start | bytes 1769480 | tf_op jit(solution)/shard_map/ppermute | solution.py:19
  4.5 2.5 %copy.66 = bf16[2,2,192,384]{3,1,0,2:T(2,128)(2,1)} copy(bf16[2,2,192,384]{3,2,1,0:T(8,128)(2,1)} %param.6) | data formatting | bytes 1179648 | tf_op args[2]
  7.0 18.6 %all-to-all-start.1 = ((bf16[2,2,192,384]{3,1,0,2:T(2,128)(2,1)}), bf16[2,2,192,384]{3,1,0,2:T(2,128)(2,1)S(1)}, u32[]{:S(2)}, u32[]{:S(2)}) async-start(bf16[2,2,192,384]{3,1,0,2:T(2,128)(2,1)} %copy.66), calls=%async_computation.1 | async-start | bytes 1179648 | tf_op jit(solution)/shard_map/all_to_all | solution.py:112
  25.8 0.9 copy-done.6
  27.0 0.4 fusion.33
  27.6 0.5 convolution_convert_fusion.2
  28.3 0.5 convolution_convert_fusion.1
  28.8 0.5 convolution_convert_fusion
  29.4 0.4 fusion.18
  30.0 0.4 fusion.21
  30.6 0.4 fusion.24
  31.0 0.4 fusion.31
  31.4 0.4 fusion.29
  31.8 0.4 fusion.27
  32.2 0.7 fusion.5
  32.9 1.4 copy.61
  34.3 28.1 %all-to-all-done.1 = bf16[2,2,192,384]{3,1,0,2:T(2,128)(2,1)S(1)} async-done(((bf16[2,2,192,384]{3,1,0,2:T(2,128)(2,1)}), bf16[2,2,192,384]{3,1,0,2:T(2,128)(2,1)S(1)}, u32[]{:S(2)}, u32[]{:S(2)}) %all-to-all-start.1) | async-done | bytes 589856 | tf_op jit(solution)/shard_map/all_to_all | solution.py:112
  62.4 6.1 %all-to-all-start = ((bf16[2,2,192,384]{3,1,0,2:T(2,128)(2,1)}), bf16[2,2,192,384]{3,1,0,2:T(2,128)(2,1)}, u32[]{:S(2)}, u32[]{:S(2)}) async-start(bf16[2,2,192,384]{3,1,0,2:T(2,128)(2,1)} %copy.61), calls=%async_computation | async-start | bytes 1179648 | tf_op jit(solution)/shard_map/all_to_all | solution.py:111
  69.1 0.3 copy.68
  69.4 0.5 reshape.142
  69.9 0.3 fusion.88
  70.3 0.5 convolution_add_fusion
  70.8 0.4 copy.70
  71.2 0.3 fusion.87
  71.5 1.3 convolution_add_fusion.1
  72.8 0.4 copy.69
  73.1 30.7 %all-to-all-done = bf16[2,2,192,384]{3,1,0,2:T(2,128)(2,1)} async-done(((bf16[2,2,192,384]{3,1,0,2:T(2,128)(2,1)}), bf16[2,2,192,384]{3,1,0,2:T(2,128)(2,1)}, u32[]{:S(2)}, u32[]{:S(2)}) %all-to-all-start) | async-done | bytes 589856 | tf_op jit(solution)/shard_map/all_to_all | solution.py:111
  103.8 2.3 %copy.63 = bf16[64,2,2,3,384]{4,3,2,1,0:T(4,128)(2,1)} copy(bf16[64,2,2,3,384]{4,2,1,3,0:T(2,128)(2,1)} %bitcast.39) | data formatting | bytes 1179648 | tf_op jit(solution)/shard_map/all_to_all | solution.py:111
  106.1 1.5 reshape.139
  107.6 0.3 fusion.86
  107.9 0.4 copy-done.3
  108.4 1.3 fusion.85
  109.7 1.6 convolution_add_fusion.2
  111.3 2.7 %copy.65 = f32[128,2304]{0,1:T(8,128)} copy(f32[128,2304]{1,0:T(8,128)} %convolution_add_fusion.2) | data formatting | bytes 2359296 | tf_op jit(solution)/shard_map/add | solution.py:60
  113.9 2.8 %convolution_add_fusion.3 = f32[128,2304]{1,0:T(8,128)} fusion(f32[128,2304]{1,0:T(8,128)} %fusion.85, bf16[128,2304]{1,0:T(8,128)(2,1)S(1)} %reshape.139, bf16[128,128]{1,0:T(8,128)(2,1)S(1)} %copy-done.3), kind=kOutput, calls=%fused_computation.3 | convolution fusion | flops 76070912 | bytes 2981888 | tf_op jit(solution)/shard_map/dot_general | solution.py:60
  116.8 2.8 %copy.64 = f32[128,2304]{0,1:T(8,128)} copy(f32[128,2304]{1,0:T(8,128)} %convolution_add_fusion.3) | data formatting | bytes 2359296 | tf_op jit(solution)/shard_map/add | solution.py:60
  119.5 1.6 multiply_subtract_fusion
  121.1 0.9 fusion.15
  122.0 0.9 fusion.16
  122.9 0.5 fusion.17
  123.4 0.3 fusion.14
  123.7 1.4 copy.71
  125.1 5.9 %all-to-all-start.2 = ((bf16[128,2,3,384]{3,1,2,0:T(2,128)(2,1)}), bf16[128,2,3,384]{3,1,2,0:T(2,128)(2,1)S(1)}, u32[]{:S(2)}, u32[]{:S(2)}) async-start(bf16[128,2,3,384]{3,1,2,0:T(2,128)(2,1)} %copy.71), calls=%async_computation.2 | async-start | bytes 1179648 | tf_op jit(solution)/shard_map/all_to_all | solution.py:115
  131.0 34.7 %all-to-all-done.2 = bf16[128,2,3,384]{3,1,2,0:T(2,128)(2,1)S(1)} async-done(((bf16[128,2,3,384]{3,1,2,0:T(2,128)(2,1)}), bf16[128,2,3,384]{3,1,2,0:T(2,128)(2,1)S(1)}, u32[]{:S(2)}, u32[]{:S(2)}) %all-to-all-start.2) | async-done | bytes 589856 | tf_op jit(solution)/shard_map/all_to_all | solution.py:115
  165.7 0.4 copy.72
  166.1 0.6 broadcast_multiply_fusion
  166.7 0.9 copy.73
  (26 shorter events, 1.6 us)
Async XLA Ops:
  0.0 25.6 %copy-start.1 = (bf16[2,3,192,384]{3,2,1,0:T(8,128)(2,1)S(1)}, bf16[2,3,192,384]{3,2,1,0:T(8,128)(2,1)}, u32[]{:S(2)}) copy-start(bf16[2,3,192,384]{3,2,1,0:T(8,128)(2,1)} %param.4) | copy-start | bytes 2654212
  0.0 25.7 %collective-permute-start.1 = (bf16[2,2,192,384]{3,2,1,0:T(8,128)(2,1)}, bf16[2,2,192,384]{3,2,1,0:T(8,128)(2,1)S(1)}, u32[]{:S(2)}, u32[]{:S(2)}) collective-permute-start(bf16[2,2,192,384]{3,2,1,0:T(8,128)(2,1)} %param.5), channel_id=1, source_target_pairs={{64,0},{128,64},{192,128},{256,192},{320,256},{384,320},{448,384},... | collective-permute-start | bytes 1769480 | tf_op jit(solution)/shard_map/ppermute | solution.py:21
  1.4 24.3 %collective-permute-start = (bf16[2,2,192,384]{3,2,1,0:T(8,128)(2,1)}, bf16[2,2,192,384]{3,2,1,0:T(8,128)(2,1)S(1)}, u32[]{:S(2)}, u32[]{:S(2)}) collective-permute-start(bf16[2,2,192,384]{3,2,1,0:T(8,128)(2,1)} %param.5), channel_id=1, source_target_pairs={{0,64},{64,128},{128,192},{192,256},{256,320},{320,384},{384,448},... | collective-permute-start | bytes 1769480 | tf_op jit(solution)/shard_map/ppermute | solution.py:19
  7.0 55.4 %all-to-all-start.1 = ((bf16[2,2,192,384]{3,1,0,2:T(2,128)(2,1)}), bf16[2,2,192,384]{3,1,0,2:T(2,128)(2,1)S(1)}, u32[]{:S(2)}, u32[]{:S(2)}) async-start(bf16[2,2,192,384]{3,1,0,2:T(2,128)(2,1)} %copy.66), calls=%async_computation.1 | async-start | bytes 1179648 | tf_op jit(solution)/shard_map/all_to_all | solution.py:112
  25.6 1.1 copy-start.6
  62.4 41.4 %all-to-all-start = ((bf16[2,2,192,384]{3,1,0,2:T(2,128)(2,1)}), bf16[2,2,192,384]{3,1,0,2:T(2,128)(2,1)}, u32[]{:S(2)}, u32[]{:S(2)}) async-start(bf16[2,2,192,384]{3,1,0,2:T(2,128)(2,1)} %copy.61), calls=%async_computation | async-start | bytes 1179648 | tf_op jit(solution)/shard_map/all_to_all | solution.py:111
  68.8 1.5 copy-start.4
  69.1 2.1 %copy-start.2 = (bf16[128,128]{1,0:T(8,128)(2,1)}, bf16[128,128]{1,0:T(8,128)(2,1)S(1)}, u32[]{:S(2)}) copy-start(bf16[128,128]{1,0:T(8,128)(2,1)S(1)} %fusion.47) | copy-start | bytes 98308
  103.8 3.8 %copy-start.5 = (bf16[128,128]{1,0:T(8,128)(2,1)S(1)}, bf16[128,128]{1,0:T(8,128)(2,1)}, u32[]{:S(2)}) copy-start(bf16[128,128]{1,0:T(8,128)(2,1)} %copy-done.4) | copy-start | bytes 98308
  107.6 0.8 copy-start.3
  116.8 2.8 %copy-start = (f32[128,2304]{0,1:T(8,128)S(1)}, f32[128,2304]{0,1:T(8,128)}, u32[]{:S(2)}) copy-start(f32[128,2304]{0,1:T(8,128)} %copy.65) | copy-start | bytes 3538948
  123.6 7.4 %copy-start.7 = (s32[192]{0:T(256)S(1)}, s32[192]{0:T(256)}, u32[]{:S(2)}) copy-start(s32[192]{0:T(256)} %param.7) | copy-start | bytes 2308
  125.1 40.6 %all-to-all-start.2 = ((bf16[128,2,3,384]{3,1,2,0:T(2,128)(2,1)}), bf16[128,2,3,384]{3,1,2,0:T(2,128)(2,1)S(1)}, u32[]{:S(2)}, u32[]{:S(2)}) async-start(bf16[128,2,3,384]{3,1,2,0:T(2,128)(2,1)} %copy.71), calls=%async_computation.2 | async-start | bytes 1179648 | tf_op jit(solution)/shard_map/all_to_all | solution.py:115
where the time goes:
time: 169 us; the launch traced here: 168 us
  waiting for transfers between devices  93.5 us (55%)
  starting transfers between devices  35.1 us (21%)
  local copies, waits for them, and re-layouts  19.2 us (11%)
  matrix products  14.3 us (8%)
  other arithmetic  5.2 us (3%)
    all_to_all x1, waiting for transfers between devices, local(): lax.all_to_all(sigma, 'energy', split_axis=0, concat_axis=2, tiled=True)  34.7 us
    all_to_all x1, waiting for transfers between devices, local(): lax.all_to_all(green, 'energy', split_axis=2, concat_axis=0, tiled=True)  30.7 us
    all_to_all x1, waiting for transfers between devices, local(): lax.all_to_all(screened, 'energy', split_axis=2, concat_axis=0, tiled=True)  28.1 us
    all_to_all x1, starting transfers between devices, local(): lax.all_to_all(screened, 'energy', split_axis=2, concat_axis=0, tiled=True)  18.6 us
    dot_general x4, matrix products, apply_split(): jnp.dot(low_part, flat, preferred_element_type=jnp.float32)  6.22 us
    add x4, local copies, waits for them, and re-layouts, apply_split(): first_pass + jnp.dot(low_part, flat, preferred_element_type=jnp.float32)  6.16 us
    all_to_all x1, starting transfers between devices, local(): lax.all_to_all(green, 'energy', split_axis=2, concat_axis=0, tiled=True)  6.1 us
    all_to_all x1, starting transfers between devices, local(): lax.all_to_all(sigma, 'energy', split_axis=0, concat_axis=2, tiled=True)  5.93 us
  transfers between devices with their start and end apart: 5, of which 3 were waited for; matrix products, arithmetic and copies ran while one was open for 9% of the time, Pallas kernels for 0%

commit v1 on v0

v1 whole, which is shorter than its diff:
```python
import math

import jax
import jax.numpy as jnp
import numpy as np
from jax import lax
from jax.experimental import pallas as pl
from jax.experimental.pallas import tpu as pltpu
from jax.sharding import PartitionSpec as P

B = 192
LIVE = 128
ENERGIES = 128
GROUPS = 64
CHUNK = 8
PACKED = GROUPS * CHUNK
F32 = jnp.float32
BF16 = jnp.bfloat16


def iota(shape, dim):
    return lax.broadcasted_iota(jnp.int32, shape, dim)


def ones_where(condition):
    return jnp.where(condition, 1.0, 0.0).astype(BF16)


def rank_row(pattern):
    live = jnp.broadcast_to(pattern, (16, B)) == 1
    upto = ones_where(iota((B, B), 0) <= iota((B, B), 1))
    count = jnp.dot(ones_where(live), upto, preferred_element_type=F32)
    return jnp.where(live, count - 1.0, -1.0).astype(jnp.int32)[:1]


def rank_column(pattern):
    live = jnp.broadcast_to(pattern, (B, 128)) == 1
    upto = ones_where(iota((B, B), 1) <= iota((B, B), 0))
    count = jnp.dot(upto, ones_where(live), preferred_element_type=F32)
    return jnp.where(live, count - 1.0, -1.0).astype(jnp.int32)[:, :1]


def pack_kernel(pattern_ref, screened_ref, out_ref):
    rank = rank_row(pattern_ref[...])
    place = iota((PACKED, 1), 0)
    wanted = (place % 2) * GROUPS + place // CHUNK
    owner = (place % CHUNK) // 2
    total = jnp.zeros((PACKED, 2 * B), F32)
    for block in range(4):
        target = jnp.where(owner == block, wanted, -2)
        select = ones_where(rank == target)
        total += jnp.dot(select, screened_ref[block], preferred_element_type=F32)
    out_ref[...] = total.astype(BF16).reshape(GROUPS, CHUNK, 2 * B)


def green_kernel(pattern_ref, retarded_ref, left_ref, own_ref, right_ref, out_ref, green_ref):
    rank = rank_row(pattern_ref[...])
    select = ones_where(rank == iota((LIVE, 1), 0))
    for energy in range(2):
        total = jnp.zeros((2 * LIVE, 2 * B), F32)
        for offset, inject_ref in enumerate((left_ref, own_ref, right_ref)):
            rows = retarded_ref[energy, offset]
            live_rows = jnp.dot(select, rows, preferred_element_type=F32).astype(BF16)
            firsts = []
            for kind in range(2):
                inject = inject_ref[energy, kind]
                lower = jnp.concatenate([-inject[:, B:], inject[:, :B]], 1)
                stacked = jnp.concatenate([inject, lower], 0)
                firsts.append(
                    jnp.dot(live_rows, stacked, preferred_element_type=F32).astype(BF16)
                )
            first = jnp.concatenate(firsts, 0)
            turned = jnp.concatenate([-rows[:, B:], rows[:, :B]], 1)
            both = jnp.concatenate([rows, turned], 0)
            total += lax.dot_general(
                first, both, (((1,), (1,)), ((), ())), preferred_element_type=F32
            )
        green_ref[energy * 2 * LIVE : (energy + 1) * 2 * LIVE, :] = total.astype(BF16)
    place = iota((PACKED, 1), 0)
    source = (place % CHUNK) * GROUPS + place // CHUNK
    order = ones_where(iota((PACKED, PACKED), 1) == source)
    packed = jnp.dot(order, green_ref[...], preferred_element_type=F32)
    out_ref[...] = packed.astype(BF16).reshape(GROUPS, CHUNK, 2 * B)


def convolve_kernel(high_ref, low_ref, green_ref, screen_ref, out_ref):
    place = iota((PACKED, 1), 0)
    energy = place % ENERGIES
    source = (energy // 2) * CHUNK + (energy % 2) * 4 + place // ENERGIES
    order = ones_where(iota((PACKED, PACKED), 1) == source)
    high, low = high_ref[...], low_ref[...]

    def ordered(ref):
        cells = ref[...].reshape(PACKED, 2 * B)
        real = jnp.dot(order, cells[:, :B], preferred_element_type=F32).astype(BF16)
        imag = jnp.dot(order, cells[:, B:], preferred_element_type=F32).astype(BF16)
        return real, imag

    def forward(real, imag, at):
        rows = slice(at * ENERGIES, (at + 1) * ENERGIES)
        stacked = jnp.concatenate([real[rows], imag[rows]], 0)
        out = jnp.dot(high, stacked, preferred_element_type=F32)
        out += jnp.dot(low, stacked, preferred_element_type=F32)
        return out[:ENERGIES], out[ENERGIES:]

    green = ordered(green_ref)
    screen = ordered(screen_ref)
    factor = 1.0 / (ENERGIES * math.sqrt(ENERGIES))
    reals, imags = [], []
    for at in range(4):
        gr, gi = forward(*green, at)
        wr, wi = forward(*screen, at)
        prod = jnp.concatenate([gr * wr - gi * wi, -(gr * wi + gi * wr)], 0)
        prod_high = prod.astype(BF16)
        prod_low = (prod - prod_high.astype(F32)).astype(BF16)
        out = jnp.dot(high, prod_high, preferred_element_type=F32)
        out += jnp.dot(high, prod_low, preferred_element_type=F32)
        out += jnp.dot(low, prod_high, preferred_element_type=F32)
        out = (out * factor).astype(BF16)
        imags.append(out[:ENERGIES])
        reals.append(out[ENERGIES:])
    place = iota((PACKED, 1), 0)
    back = (place % 4) * ENERGIES + (place // CHUNK) * 2 + (place // 4) % 2
    order = ones_where(iota((PACKED, PACKED), 1) == back)
    real = jnp.dot(order, jnp.concatenate(reals, 0), preferred_element_type=F32)
    imag = jnp.dot(order, jnp.concatenate(imags, 0), preferred_element_type=F32)
    out_ref[...] = jnp.concatenate([real, imag], 1).astype(BF16).reshape(GROUPS, CHUNK, 2 * B)


def expand_kernel(pattern_ref, packed_ref, out_ref):
    rank = rank_column(pattern_ref[...])
    place = iota((1, PACKED), 1)
    holds = (place % 2) * GROUPS + place // CHUNK
    owner = (place % CHUNK) // 2
    packed = packed_ref[...].reshape(PACKED, 2 * B)
    for block in range(4):
        select = ones_where(rank == jnp.where(owner == block, holds, -2))
        out_ref[block] = jnp.dot(select, packed, preferred_element_type=F32).astype(BF16)


def tables():
    index = np.arange(ENERGIES)
    angle = 2.0 * np.pi / ENERGIES * (index[:, None] * index[None, :] % ENERGIES)
    cosine, sine = np.cos(angle), np.sin(angle)
    whole = np.block([[cosine, sine], [-sine, cosine]]).astype(np.float32)
    high = whole.astype(BF16)
    low = (whole - high.astype(np.float32)).astype(BF16)
    return jnp.asarray(high), jnp.asarray(low)


def call(kernel, shape, *operands, scratch=()):
    return pl.pallas_call(
        kernel,
        out_shape=jax.ShapeDtypeStruct(shape, BF16),
        scratch_shapes=scratch,
        compiler_params=pltpu.CompilerParams(vmem_limit_bytes=48 << 20),
    )(*operands)


def exchange(packed):
    return lax.all_to_all(packed, "energy", split_axis=0, concat_axis=0, tiled=True)


def local(retarded, injection, screened, pattern):
    packed_shape = (GROUPS, CHUNK, 2 * B)
    row, column = pattern.reshape(1, B), pattern.reshape(B, 1)
    count = lax.axis_size("slab")
    up = [(i, i + 1) for i in range(count - 1)]
    left = lax.ppermute(injection, "slab", up)
    right = lax.ppermute(injection, "slab", [(b, a) for a, b in up])
    screen = call(pack_kernel, packed_shape, row, screened.reshape(4, B, 2 * B))
    screen = exchange(screen)
    green = call(
        green_kernel,
        packed_shape,
        row,
        retarded,
        left,
        injection,
        right,
        scratch=[pltpu.VMEM((PACKED, 2 * B), BF16)],
    )
    green = exchange(green)
    sigma = call(convolve_kernel, packed_shape, *tables(), green, screen)
    sigma = exchange(sigma)
    out = call(expand_kernel, (4, B, 2 * B), column, sigma)
    return out.reshape(2, 2, B, 2 * B)


def solution(mesh):
    placed = P("energy", None, "slab", None)
    return jax.shard_map(
        local,
        mesh=mesh,
        in_specs=(placed, placed, placed, P("slab")),
        out_specs=placed,
        check_vma=False,
    )
```

time: 169 us -> 121 us (0.72)
  the two profiles are of different devices: /device:TPU:16 before, /device:TPU:2 now
where the time goes in v1:
time: 121 us
  waiting for transfers between devices  45.3 us (37%)
  blocking collectives  33.4 us (28%)
  starting transfers between devices  30.3 us (25%)
  Pallas kernels  10.1 us (8%)
  local copies, waits for them, and re-layouts  1.88 us (2%)
    all_to_all x2, waiting for transfers between devices, exchange(): lax.all_to_all(packed, 'energy', split_axis=0, concat_axis=0, tiled=True)  37.9 us
    all_to_all x1, blocking collectives, exchange(): lax.all_to_all(packed, 'energy', split_axis=0, concat_axis=0, tiled=True)  33.4 us
    all_to_all x2, starting transfers between devices, exchange(): lax.all_to_all(packed, 'energy', split_axis=0, concat_axis=0, tiled=True)  24.7 us
    pallas_call x4, Pallas kernels, call(): pl.pallas_call(kernel, out_shape=jax.ShapeDtypeStruct(shape, BF16), scrat...  10.1 us
    ppermute x1, waiting for transfers between devices, local(): left = lax.ppermute(injection, 'slab', up)  5.62 us
    ppermute x1, starting transfers between devices, local(): right = lax.ppermute(injection, 'slab', [(b, a) for a, b in up])  3.64 us
  transfers between devices with their start and end apart: 4, of which 4 were waited for; matrix products, arithmetic and copies ran while one was open for 0% of the time, Pallas kernels for 3%

profile of v1, /device:TPU:2, one launch (start us, length us, event | category | flops | bytes accessed | tf_op | source)
XLA Modules:
  0.0 121.1 jit_solution(8876293548274649653)
XLA Ops:
  0.0 0.0 copy-start.5
  0.0 0.7 copy-done.5
  0.7 0.0 copy-start.1
  0.7 1.1 copy-done.1
  1.7 0.0 copy-start
  1.7 1.6 %shard_map.65 = bf16[64,8,384]{2,1,0:T(8,128)(2,1)} custom-call(s32[1,192]{1,0:T(1,128)S(1)} %bitcast.5, bf16[4,192,384]{2,1,0:T(8,128)(2,1)S(1)} %bitcast.4), custom_call_target="tpu_custom_call" | custom-call | tf_op jit(solution)/shard_map/pallas_call | solution.py:152
  3.4 0.0 copy-start.2
  3.4 18.9 %all-to-all-start.1 = ((bf16[64,8,384]{2,1,0:T(8,128)(2,1)}), bf16[64,8,384]{2,1,0:T(8,128)(2,1)S(1)}, u32[]{:S(2)}, u32[]{:S(2)}) async-start(bf16[64,8,384]{2,1,0:T(8,128)(2,1)} %shard_map.65), calls=%async_computation.1 | async-start | bytes 786432 | tf_op jit(solution)/shard_map/all_to_all | solution.py:161
  22.2 0.0 copy-done.2
  22.2 1.9 %collective-permute-start = (bf16[2,2,192,384]{3,2,1,0:T(8,128)(2,1)S(1)}, bf16[2,2,192,384]{3,2,1,0:T(8,128)(2,1)S(1)}, u32[]{:S(2)}, u32[]{:S(2)}) collective-permute-start(bf16[2,2,192,384]{3,2,1,0:T(8,128)(2,1)S(1)} %copy-done.2), channel_id=1, source_target_pairs={{0,64},{64,128},{128,192},{192,256},{256,320},{320,384},{384,448},... | collective-permute-start | bytes 1769480 | tf_op jit(solution)/shard_map/ppermute | solution.py:169
  24.2 3.6 %collective-permute-start.1 = (bf16[2,2,192,384]{3,2,1,0:T(8,128)(2,1)S(1)}, bf16[2,2,192,384]{3,2,1,0:T(8,128)(2,1)S(1)}, u32[]{:S(2)}, u32[]{:S(2)}) collective-permute-start(bf16[2,2,192,384]{3,2,1,0:T(8,128)(2,1)S(1)} %copy-done.2), channel_id=1, source_target_pairs={{64,0},{128,64},{192,128},{256,192},{320,256},{384,320},{448,384},... | collective-permute-start | bytes 1769480 | tf_op jit(solution)/shard_map/ppermute | solution.py:170
  27.8 5.6 %collective-permute-done.left_ref = bf16[2,2,192,384]{3,2,1,0:T(8,128)(2,1)S(1)} collective-permute-done((bf16[2,2,192,384]{3,2,1,0:T(8,128)(2,1)S(1)}, bf16[2,2,192,384]{3,2,1,0:T(8,128)(2,1)S(1)}, u32[]{:S(2)}, u32[]{:S(2)}) %collective-permute-start) | collective-permute-done | bytes 589856 | tf_op jit(solution)/shard_map/ppermute | solution.py:169
  33.4 1.8 %collective-permute-done.1.right_ref = bf16[2,2,192,384]{3,2,1,0:T(8,128)(2,1)S(1)} collective-permute-done((bf16[2,2,192,384]{3,2,1,0:T(8,128)(2,1)S(1)}, bf16[2,2,192,384]{3,2,1,0:T(8,128)(2,1)S(1)}, u32[]{:S(2)}, u32[]{:S(2)}) %collective-permute-start.1) | collective-permute-done | bytes 589856 | tf_op jit(solution)/shard_map/ppermute | solution.py:170
  35.2 0.0 copy-done
  35.2 3.2 %shard_map.64 = bf16[64,8,384]{2,1,0:T(8,128)(2,1)S(1)} custom-call(s32[1,192]{1,0:T(1,128)S(1)} %bitcast.6, bf16[2,3,192,384]{3,2,1,0:T(8,128)(2,1)S(1)} %copy-done, bf16[2,2,192,384]{3,2,1,0:T(8,128)(2,1)S(1)} %collective-permute-done.left_ref, bf16[2,2,192,384]{3,2,1,0:T(8,128)(2,1)S(1)} %copy-done.2, ...), custom_call_target="tpu_custom_call" | custom-call | tf_op jit(solution)/shard_map/pallas_call | solution.py:152
  38.4 0.0 copy-start.3
  38.4 0.0 copy-start.4
  38.4 11.0 %all-to-all-done.1.screen_ref = bf16[64,8,384]{2,1,0:T(8,128)(2,1)S(1)} async-done(((bf16[64,8,384]{2,1,0:T(8,128)(2,1)}), bf16[64,8,384]{2,1,0:T(8,128)(2,1)S(1)}, u32[]{:S(2)}, u32[]{:S(2)}) %all-to-all-start.1) | async-done | bytes 393248 | tf_op jit(solution)/shard_map/all_to_all | solution.py:161
  49.4 33.4 %all_to_all.15.green_ref = bf16[64,8,384]{2,1,0:T(8,128)(2,1)S(1)} all-to-all(bf16[64,8,384]{2,1,0:T(8,128)(2,1)S(1)} %shard_map.64), channel_id=1, replica_groups=mesh['slab'=8,'energy'=64] {'energy'}, dimensions={0} | all-to-all | bytes 786432 | tf_op jit(solution)/shard_map/all_to_all | solution.py:161
  82.9 0.0 copy-done.3
  82.9 0.0 copy-done.4
  82.9 3.6 %shard_map.66 = bf16[64,8,384]{2,1,0:T(8,128)(2,1)} custom-call(bf16[256,256]{1,0:T(8,128)(2,1)S(1)} %copy-done.3, bf16[256,256]{1,0:T(8,128)(2,1)S(1)} %copy-done.4, bf16[64,8,384]{2,1,0:T(8,128)(2,1)S(1)} %all_to_all.15.green_ref, bf16[64,8,384]{2,1,0:T(8,128)(2,1)S(1)} %all-to-all-done.1.screen_ref), custom_call_target="tpu_custom_call" | custom-call | tf_op jit(solution)/shard_map/pallas_call | solution.py:152
  86.5 5.8 %all-to-all-start.2 = ((bf16[64,8,384]{2,1,0:T(8,128)(2,1)}), bf16[64,8,384]{2,1,0:T(8,128)(2,1)S(1)}, u32[]{:S(2)}, u32[]{:S(2)}) async-start(bf16[64,8,384]{2,1,0:T(8,128)(2,1)} %shard_map.66), calls=%async_computation.2 | async-start | bytes 786432 | tf_op jit(solution)/shard_map/all_to_all | solution.py:161
  92.4 0.1 copy.7.pattern_ref
  92.5 26.9 %all-to-all-done.2.packed_ref = bf16[64,8,384]{2,1,0:T(8,128)(2,1)S(1)} async-done(((bf16[64,8,384]{2,1,0:T(8,128)(2,1)}), bf16[64,8,384]{2,1,0:T(8,128)(2,1)S(1)}, u32[]{:S(2)}, u32[]{:S(2)}) %all-to-all-start.2) | async-done | bytes 393248 | tf_op jit(solution)/shard_map/all_to_all | solution.py:161
  119.4 1.7 %shard_map.67 = bf16[4,192,384]{2,1,0:T(8,128)(2,1)} custom-call(s32[192,1]{1,0:T(8,128)S(1)} %copy.7.pattern_ref, bf16[64,8,384]{2,1,0:T(8,128)(2,1)S(1)} %all-to-all-done.2.packed_ref), custom_call_target="tpu_custom_call" | custom-call | tf_op jit(solution)/shard_map/pallas_call | solution.py:152
Async XLA Ops:
  0.0 0.7 copy-start.5
  0.7 1.1 copy-start.1
  1.7 33.4 %copy-start = (bf16[2,3,192,384]{3,2,1,0:T(8,128)(2,1)S(1)}, bf16[2,3,192,384]{3,2,1,0:T(8,128)(2,1)}, u32[]{:S(2)}) copy-start(bf16[2,3,192,384]{3,2,1,0:T(8,128)(2,1)} %retarded_ref.1) | copy-start | bytes 2654212
  3.4 18.9 %copy-start.2 = (bf16[2,2,192,384]{3,2,1,0:T(8,128)(2,1)S(1)}, bf16[2,2,192,384]{3,2,1,0:T(8,128)(2,1)}, u32[]{:S(2)}) copy-start(bf16[2,2,192,384]{3,2,1,0:T(8,128)(2,1)} %own_ref.1) | copy-start | bytes 1769476
  3.4 46.1 %all-to-all-start.1 = ((bf16[64,8,384]{2,1,0:T(8,128)(2,1)}), bf16[64,8,384]{2,1,0:T(8,128)(2,1)S(1)}, u32[]{:S(2)}, u32[]{:S(2)}) async-start(bf16[64,8,384]{2,1,0:T(8,128)(2,1)} %shard_map.65), calls=%async_computation.1 | async-start | bytes 786432 | tf_op jit(solution)/shard_map/all_to_all | solution.py:161
  22.2 11.2 %collective-permute-start = (bf16[2,2,192,384]{3,2,1,0:T(8,128)(2,1)S(1)}, bf16[2,2,192,384]{3,2,1,0:T(8,128)(2,1)S(1)}, u32[]{:S(2)}, u32[]{:S(2)}) collective-permute-start(bf16[2,2,192,384]{3,2,1,0:T(8,128)(2,1)S(1)} %copy-done.2), channel_id=1, source_target_pairs={{0,64},{64,128},{128,192},{192,256},{256,320},{320,384},{384,448},... | collective-permute-start | bytes 1769480 | tf_op jit(solution)/shard_map/ppermute | solution.py:169
  24.2 11.0 %collective-permute-start.1 = (bf16[2,2,192,384]{3,2,1,0:T(8,128)(2,1)S(1)}, bf16[2,2,192,384]{3,2,1,0:T(8,128)(2,1)S(1)}, u32[]{:S(2)}, u32[]{:S(2)}) collective-permute-start(bf16[2,2,192,384]{3,2,1,0:T(8,128)(2,1)S(1)} %copy-done.2), channel_id=1, source_target_pairs={{64,0},{128,64},{192,128},{256,192},{320,256},{384,320},{448,384},... | collective-permute-start | bytes 1769480 | tf_op jit(solution)/shard_map/ppermute | solution.py:170
  38.4 44.5 %copy-start.3 = (bf16[256,256]{1,0:T(8,128)(2,1)S(1)}, bf16[256,256]{1,0:T(8,128)(2,1)}, u32[]{:S(2)}) copy-start(bf16[256,256]{1,0:T(8,128)(2,1)} %constant.4.clone.high_ref) | copy-start | bytes 393220
  38.4 44.5 %copy-start.4 = (bf16[256,256]{1,0:T(8,128)(2,1)S(1)}, bf16[256,256]{1,0:T(8,128)(2,1)}, u32[]{:S(2)}) copy-start(bf16[256,256]{1,0:T(8,128)(2,1)} %constant.5.clone.low_ref) | copy-start | bytes 393220
  86.5 32.9 %all-to-all-start.2 = ((bf16[64,8,384]{2,1,0:T(8,128)(2,1)}), bf16[64,8,384]{2,1,0:T(8,128)(2,1)S(1)}, u32[]{:S(2)}, u32[]{:S(2)}) async-start(bf16[64,8,384]{2,1,0:T(8,128)(2,1)} %shard_map.66), calls=%async_computation.2 | async-start | bytes 786432 | tf_op jit(solution)/shard_map/all_to_all | solution.py:161

commit v2 on v1

v2 whole, which is shorter than its diff:
```python
import math

import jax
import jax.numpy as jnp
import numpy as np
from jax import lax
from jax.experimental import pallas as pl
from jax.experimental.pallas import tpu as pltpu
from jax.sharding import PartitionSpec as P

B = 192
LIVE = 128
ENERGIES = 128
GROUPS = 64
CHUNK = 8
PACKED = GROUPS * CHUNK
F32 = jnp.float32
BF16 = jnp.bfloat16


def iota(shape, dim):
    return lax.broadcasted_iota(jnp.int32, shape, dim)


def ones_where(condition):
    return jnp.where(condition, 1.0, 0.0).astype(BF16)


def rank_row(pattern):
    live = jnp.broadcast_to(pattern, (16, B)) == 1
    upto = ones_where(iota((B, B), 0) <= iota((B, B), 1))
    count = jnp.dot(ones_where(live), upto, preferred_element_type=F32)
    return jnp.where(live, count - 1.0, -1.0).astype(jnp.int32)[:1]


def rank_column(pattern):
    live = jnp.broadcast_to(pattern, (B, 128)) == 1
    upto = ones_where(iota((B, B), 1) <= iota((B, B), 0))
    count = jnp.dot(upto, ones_where(live), preferred_element_type=F32)
    return jnp.where(live, count - 1.0, -1.0).astype(jnp.int32)[:, :1]


def pack_kernel(spot_ref, pattern_hbm, screened_hbm, out_ref, pattern_ref, screened_ref, sems):
    copies = [pltpu.make_async_copy(pattern_hbm, pattern_ref, sems.at[4])]
    for block in range(4):
        copies.append(
            pltpu.make_async_copy(
                screened_hbm.at[block], screened_ref.at[block], sems.at[block]
            )
        )
    for copy in copies:
        copy.start()
    place = iota((PACKED, 1), 0)
    chunk = place // CHUNK
    wanted = (place % 2) * GROUPS + (chunk // 4) * 4 + (chunk + spot_ref[0]) % 4
    owner = (place % CHUNK) // 2
    copies[0].wait()
    rank = rank_row(pattern_ref[...])
    total = jnp.zeros((PACKED, 2 * B), F32)
    for block in range(4):
        select = ones_where(rank == jnp.where(owner == block, wanted, -2))
        copies[block + 1].wait()
        total += jnp.dot(select, screened_ref[block], preferred_element_type=F32)
    out_ref[...] = total.astype(BF16).reshape(16, 4 * CHUNK, 2 * B)


def turned(cells):
    return jnp.concatenate([-cells[:, B:], cells[:, :B]], 1)


def green_term(live, rows, inject_ref, energy):
    live_rows = jnp.dot(live, rows, preferred_element_type=F32).astype(BF16)
    firsts = []
    for kind in range(2):
        inject = inject_ref[energy, kind]
        stacked = jnp.concatenate([inject, turned(inject)], 0)
        firsts.append(jnp.dot(live_rows, stacked, preferred_element_type=F32).astype(BF16))
    both = jnp.concatenate([rows, turned(rows)], 0)
    return lax.dot_general(
        jnp.concatenate(firsts, 0), both, (((1,), (1,)), ((), ())), preferred_element_type=F32
    )


def near_kernel(odd_ref, pattern_ref, retarded_ref, own_ref, near_ref, total_ref, live_ref, order_ref):
    live = ones_where(rank_row(pattern_ref[...]) == iota((LIVE, 1), 0))
    live_ref[...] = live
    side = 2 - 2 * odd_ref[0]
    for energy in range(2):
        total = green_term(live, retarded_ref[energy, 1], own_ref, energy)
        total += green_term(live, retarded_ref[energy, side], near_ref, energy)
        total_ref[energy] = total
    place = iota((PACKED, 1), 0)
    source = (place % CHUNK) * GROUPS + place // CHUNK
    order_ref[...] = ones_where(iota((PACKED, PACKED), 1) == source)


def far_kernel(odd_ref, live_ref, retarded_ref, far_ref, total_ref, order_ref, out_ref):
    side = 2 * odd_ref[0]
    live = live_ref[...]
    greens = []
    for energy in range(2):
        term = green_term(live, retarded_ref[energy, side], far_ref, energy)
        greens.append((total_ref[energy] + term).astype(BF16))
    packed = jnp.dot(order_ref[...], jnp.concatenate(greens, 0), preferred_element_type=F32)
    out_ref[...] = packed.astype(BF16).reshape(GROUPS, CHUNK, 2 * B)


def ordered(order, cells):
    real = jnp.dot(order, cells[:, :B], preferred_element_type=F32).astype(BF16)
    imag = jnp.dot(order, cells[:, B:], preferred_element_type=F32).astype(BF16)
    return real, imag


def forward(high, low, real, imag, at):
    rows = slice(at * ENERGIES, (at + 1) * ENERGIES)
    stacked = jnp.concatenate([real[rows], imag[rows]], 0)
    out = jnp.dot(high, stacked, preferred_element_type=F32)
    return out + jnp.dot(low, stacked, preferred_element_type=F32)


def screen_kernel(spot_ref, high_ref, low_ref, *refs):
    screen_refs, (out_ref, order_ref, back_ref) = refs[:4], refs[4:]
    cell = iota((1, PACKED), 1)
    within = cell % ENERGIES
    origin = (within // CHUNK) * 4 + (spot_ref[0] + 4 - cell // ENERGIES) % 4
    target = (cell % 4) * ENERGIES + origin * 2 + (cell % CHUNK) // 4
    order = ones_where(iota((PACKED, PACKED), 0) == target)
    cells = [ref[...].reshape(ENERGIES, 2 * B) for ref in screen_refs]
    real, imag = ordered(order, jnp.concatenate(cells, 0))
    for at in range(4):
        out_ref[at] = forward(high_ref[...], low_ref[...], real, imag, at)
    place = iota((PACKED, 1), 0)
    energy = place % ENERGIES
    source = (energy // 2) * CHUNK + (energy % 2) * 4 + place // ENERGIES
    order_ref[...] = ones_where(iota((PACKED, PACKED), 1) == source)
    back = (place % 4) * ENERGIES + (place // CHUNK) * 2 + (place // 4) % 2
    back_ref[...] = ones_where(iota((PACKED, PACKED), 1) == back)


def convolve_kernel(high_ref, low_ref, order_ref, back_ref, screen_ref, green_ref, out_ref):
    high, low = high_ref[...], low_ref[...]
    green = ordered(order_ref[...], green_ref[...].reshape(PACKED, 2 * B))
    factor = 1.0 / (ENERGIES * math.sqrt(ENERGIES))
    reals, imags = [], []
    for at in range(4):
        out = forward(high, low, *green, at)
        gr, gi = out[:ENERGIES], out[ENERGIES:]
        wr, wi = screen_ref[at, :ENERGIES], screen_ref[at, ENERGIES:]
        prod = jnp.concatenate([gr * wr - gi * wi, -(gr * wi + gi * wr)], 0)
        prod_high = prod.astype(BF16)
        prod_low = (prod - prod_high.astype(F32)).astype(BF16)
        out = jnp.dot(high, prod_high, preferred_element_type=F32)
        out += jnp.dot(high, prod_low, preferred_element_type=F32)
        out += jnp.dot(low, prod_high, preferred_element_type=F32)
        out = (out * factor).astype(BF16)
        imags.append(out[:ENERGIES])
        reals.append(out[ENERGIES:])
    back = back_ref[...]
    real = jnp.dot(back, jnp.concatenate(reals, 0), preferred_element_type=F32)
    imag = jnp.dot(back, jnp.concatenate(imags, 0), preferred_element_type=F32)
    out_ref[...] = jnp.concatenate([real, imag], 1).astype(BF16).reshape(GROUPS, CHUNK, 2 * B)


def select_kernel(pattern_ref, out_ref):
    rank = rank_column(pattern_ref[...])
    place = iota((1, PACKED), 1)
    holds = (place % 2) * GROUPS + place // CHUNK
    owner = (place % CHUNK) // 2
    for block in range(4):
        out_ref[block] = ones_where(rank == jnp.where(owner == block, holds, -2))


def expand_kernel(select_ref, packed_ref, out_hbm, out_ref, sems):
    packed = packed_ref[...].reshape(PACKED, 2 * B)
    copies = []
    for block in range(4):
        rows = jnp.dot(select_ref[block], packed, preferred_element_type=F32)
        out_ref[block] = rows.astype(BF16)
        copies.append(
            pltpu.make_async_copy(out_ref.at[block], out_hbm.at[block], sems.at[block])
        )
        copies[-1].start()
    for copy in copies:
        copy.wait()


def tables():
    index = np.arange(ENERGIES)
    angle = 2.0 * np.pi / ENERGIES * (index[:, None] * index[None, :] % ENERGIES)
    cosine, sine = np.cos(angle), np.sin(angle)
    whole = np.block([[cosine, sine], [-sine, cosine]]).astype(np.float32)
    high = whole.astype(BF16)
    low = (whole - high.astype(np.float32)).astype(BF16)
    return jnp.asarray(high), jnp.asarray(low)


VMEM, SMEM, HBM = pltpu.VMEM, pltpu.SMEM, pltpu.HBM


def call(kernel, outs, *operands, spaces=None, out_space=VMEM, scratch=(), room=48):
    spaces = spaces or [VMEM] * len(operands)
    return pl.pallas_call(
        kernel,
        in_specs=[pl.BlockSpec(memory_space=space) for space in spaces],
        out_specs=jax.tree.map(lambda _: pl.BlockSpec(memory_space=out_space), outs),
        out_shape=outs,
        scratch_shapes=scratch,
        compiler_params=pltpu.CompilerParams(vmem_limit_bytes=room << 20),
    )(*operands)


def array(shape, kind=BF16):
    return jax.ShapeDtypeStruct(shape, kind)


def exchange(packed, groups=None):
    return lax.all_to_all(
        packed, "energy", split_axis=0, concat_axis=0, tiled=True, axis_index_groups=groups
    )


def swapped(cells, pairs):
    return lax.ppermute(cells, "slab", pairs + [(b, a) for a, b in pairs])


def local(retarded, injection, screened, pattern):
    packed = array((GROUPS, CHUNK, 2 * B))
    row, column = pattern.reshape(1, B), pattern.reshape(B, 1)
    spot = (lax.axis_index("energy") & 3).reshape(1)
    high, low = tables()
    screen = call(
        pack_kernel,
        array((16, 4 * CHUNK, 2 * B)),
        spot,
        row,
        screened.reshape(4, B, 2 * B),
        spaces=[SMEM, HBM, HBM],
        room=64,
        scratch=[
            VMEM((1, B), jnp.int32),
            VMEM((4, B, 2 * B), BF16),
            pltpu.SemaphoreType.DMA((5,)),
        ],
    )
    with jax.named_scope("screens"):
        screen = exchange(screen, [[4 * z + y for z in range(16)] for y in range(4)])
    count = lax.axis_size("slab")
    odd = (lax.axis_index("slab") & 1).reshape(1)
    with jax.named_scope("halo"):
        far = swapped(injection, [(i, i + 1) for i in range(1, count - 1, 2)])
        near = swapped(injection, [(i, i + 1) for i in range(0, count, 2)])
    total, live, order = call(
        near_kernel,
        [array((2, 2 * LIVE, 2 * B), F32), array((LIVE, B)), array((PACKED, PACKED))],
        odd,
        row,
        retarded,
        injection,
        near,
        spaces=[SMEM] + [VMEM] * 4,
    )
    green = call(
        far_kernel,
        packed,
        odd,
        live,
        retarded,
        far,
        total,
        order,
        spaces=[SMEM] + [VMEM] * 5,
    )
    with jax.named_scope("greens"):
        green = exchange(green)
    screen = screen.reshape(16, 4, CHUNK, 2 * B)
    with jax.named_scope("side"):
        screen = [screen[:, 0]] + [
            lax.ppermute(
                screen[:, step],
                "energy",
                [(4 * z + y, 4 * z + (y + step) % 4) for z in range(16) for y in range(4)],
            )
            for step in range(1, 4)
        ]
    with jax.named_scope("early"):
        screen, order, back = call(
            screen_kernel,
            [
                array((4, 2 * ENERGIES, B), F32),
                array((PACKED, PACKED)),
                array((PACKED, PACKED)),
            ],
            spot,
            high,
            low,
            *screen,
            spaces=[SMEM] + [VMEM] * 6,
        )
    sigma = call(convolve_kernel, packed, high, low, order, back, screen, green)
    with jax.named_scope("sigmas"):
        sigma = exchange(sigma)
    select = call(select_kernel, array((4, B, PACKED)), column)
    out = call(
        expand_kernel,
        array((4, B, 2 * B)),
        select,
        sigma,
        out_space=HBM,
        scratch=[VMEM((4, B, 2 * B), BF16), pltpu.SemaphoreType.DMA((4,))],
    )
    return out.reshape(2, 2, B, 2 * B)


def solution(mesh):
    placed = P("energy", None, "slab", None)
    return jax.shard_map(
        local,
        mesh=mesh,
        in_specs=(placed, placed, placed, P("slab")),
        out_specs=placed,
        check_vma=False,
    )
```

time: 121 us -> 116 us (0.959)
  the two profiles are of different devices: /device:TPU:2 before, /device:TPU:4 now
where the time goes in v2:
time: 116 us; the launch traced here: 115 us
  waiting for transfers between devices  55.5 us (48%)
  starting transfers between devices  45.2 us (39%)
  Pallas kernels  12.6 us (11%)
  local copies, waits for them, and re-layouts  2.01 us (2%)
    all_to_all x3, waiting for transfers between devices, exchange(): lax.all_to_all(packed, 'energy', split_axis=0, concat_axis=0, tiled=True,...  45.3 us
    all_to_all x3, starting transfers between devices, exchange(): lax.all_to_all(packed, 'energy', split_axis=0, concat_axis=0, tiled=True,...  30.3 us
    pallas_call x7, Pallas kernels, call(): pl.pallas_call(kernel, in_specs=[pl.BlockSpec(memory_space=space) for spa...  12.6 us
    ppermute x3, starting transfers between devices, local(): lax.ppermute(screen[:, step], 'energy', [(4 * z + y, 4 * z + (y + step) %...  10.4 us
    ppermute x3, waiting for transfers between devices, local(): lax.ppermute(screen[:, step], 'energy', [(4 * z + y, 4 * z + (y + step) %...  5.62 us
    ppermute x2, waiting for transfers between devices, swapped(): return lax.ppermute(cells, 'slab', pairs + [(b, a) for a, b in pairs])  4.61 us
    ppermute x2, starting transfers between devices, swapped(): return lax.ppermute(cells, 'slab', pairs + [(b, a) for a, b in pairs])  4.47 us
  transfers between devices with their start and end apart: 8, of which 6 were waited for; matrix products, arithmetic and copies ran while one was open for 0% of the time, Pallas kernels for 5%

profile of v2, /device:TPU:4, one launch (start us, length us, event | category | flops | bytes accessed | tf_op | source)
XLA Modules:
  0.0 115.4 jit_solution(3467465277751618854)
XLA Ops:
  0.0 2.7 %shard_map.65 = bf16[16,32,384]{2,1,0:T(8,128)(2,1)} custom-call(s32[1]{0:T(128)} %bitcast.1.spot_ref, s32[1,192]{1,0:T(1,128)} %bitcast.23, bf16[4,192,384]{2,1,0:T(8,128)(2,1)} %bitcast.27), custom_call_target="tpu_custom_call" | custom-call | tf_op jit(solution)/shard_map/pallas_call | solution.py:202
  2.7 0.0 copy-start.2
  2.7 15.3 %all-to-all-start = ((bf16[16,32,384]{2,1,0:T(8,128)(2,1)}), bf16[16,32,384]{2,1,0:T(8,128)(2,1)S(1)}, u32[]{:S(2)}, u32[]{:S(2)}) async-start(bf16[16,32,384]{2,1,0:T(8,128)(2,1)} %shard_map.65), calls=%async_computation | async-start | bytes 786432 | tf_op jit(solution)/shard_map/screens/all_to_all | solution.py:217
  18.1 0.0 copy-done.2
  18.1 1.9 %collective-permute-start.3 = (bf16[2,2,192,384]{3,2,1,0:T(8,128)(2,1)S(1)}, bf16[2,2,192,384]{3,2,1,0:T(8,128)(2,1)S(1)}, u32[]{:S(2)}, u32[]{:S(2)}) collective-permute-start(bf16[2,2,192,384]{3,2,1,0:T(8,128)(2,1)S(1)} %copy-done.2), channel_id=1, source_target_pairs={{0,64},{128,192},{256,320},{384,448},{64,0},{192,128},{320,256},{4... | collective-permute-start | bytes 1769480 | tf_op jit(solution)/shard_map/halo/ppermute | solution.py:223
  20.0 2.5 %collective-permute-start.4 = (bf16[2,2,192,384]{3,2,1,0:T(8,128)(2,1)S(1)}, bf16[2,2,192,384]{3,2,1,0:T(8,128)(2,1)S(1)}, u32[]{:S(2)}, u32[]{:S(2)}) collective-permute-start(bf16[2,2,192,384]{3,2,1,0:T(8,128)(2,1)S(1)} %copy-done.2), channel_id=1, source_target_pairs={{64,128},{192,256},{320,384},{128,64},{256,192},{384,320},{65,129}... | collective-permute-start | bytes 1769480 | tf_op jit(solution)/shard_map/halo/ppermute | solution.py:223
  22.6 0.0 copy-start.5
  22.6 0.0 collective-permute-done.3.near_ref
  22.6 0.7 copy-done.5
  23.2 0.0 copy-start
  23.2 1.2 %copy-done = bf16[2,3,192,384]{3,2,1,0:T(8,128)(2,1)S(1)} copy-done((bf16[2,3,192,384]{3,2,1,0:T(8,128)(2,1)S(1)}, bf16[2,3,192,384]{3,2,1,0:T(8,128)(2,1)}, u32[]{:S(2)}) %copy-start) | copy-done | bytes 884760
  24.4 0.0 copy-start.1
  24.4 2.2 %shard_map.66 = (f32[2,256,384]{2,1,0:T(8,128)S(1)}, bf16[128,192]{1,0:T(8,128)(2,1)S(1)}, bf16[512,512]{1,0:T(8,128)(2,1)S(1)}) custom-call(s32[1]{0:T(128)} %bitcast.9.odd_ref, s32[1,192]{1,0:T(1,128)S(1)} %bitcast.24, bf16[2,3,192,384]{3,2,1,0:T(8,128)(2,1)S(1)} %copy-done, bf16[2,2,192,384]{3,2,1,0:T(8,128)(2,1)S(1)} %copy-done.2, ...), custom_call_target="tpu_custom_call" | custom-call | tf_op jit(solution)/shard_map/pallas_call | solution.py:202
  26.6 4.6 %collective-permute-done.4.far_ref = bf16[2,2,192,384]{3,2,1,0:T(8,128)(2,1)S(1)} collective-permute-done((bf16[2,2,192,384]{3,2,1,0:T(8,128)(2,1)S(1)}, bf16[2,2,192,384]{3,2,1,0:T(8,128)(2,1)S(1)}, u32[]{:S(2)}, u32[]{:S(2)}) %collective-permute-start.4) | collective-permute-done | bytes 589856 | tf_op jit(solution)/shard_map/halo/ppermute | solution.py:223
  31.2 0.0 copy-done.1
  31.2 2.1 %shard_map.67 = bf16[64,8,384]{2,1,0:T(8,128)(2,1)} custom-call(s32[1]{0:T(128)} %bitcast.9.odd_ref, bf16[128,192]{1,0:T(8,128)(2,1)S(1)} %get-tuple-element.14.live_ref, bf16[2,3,192,384]{3,2,1,0:T(8,128)(2,1)S(1)} %copy-done.1, bf16[2,2,192,384]{3,2,1,0:T(8,128)(2,1)S(1)} %collective-permute-done.4.far_ref, ...), custom_call_target="tpu_custom_call" | custom-call | tf_op jit(solution)/shard_map/pallas_call | solution.py:202
  33.3 8.5 %all-to-all-done = bf16[16,32,384]{2,1,0:T(8,128)(2,1)S(1)} async-done(((bf16[16,32,384]{2,1,0:T(8,128)(2,1)}), bf16[16,32,384]{2,1,0:T(8,128)(2,1)S(1)}, u32[]{:S(2)}, u32[]{:S(2)}) %all-to-all-start) | async-done | bytes 393248 | tf_op jit(solution)/shard_map/screens/all_to_all | solution.py:217
  41.9 9.5 %all-to-all-start.1 = ((bf16[64,8,384]{2,1,0:T(8,128)(2,1)}), bf16[64,8,384]{2,1,0:T(8,128)(2,1)S(1)}, u32[]{:S(2)}, u32[]{:S(2)}) async-start(bf16[64,8,384]{2,1,0:T(8,128)(2,1)} %shard_map.67), calls=%async_computation.1 | async-start | bytes 786432 | tf_op jit(solution)/shard_map/greens/all_to_all | solution.py:217
  51.4 0.0 copy-start.3
  51.4 0.0 copy-start.4
  51.5 4.8 %collective-permute-start.2 = (bf16[16,8,384]{2,1,0:T(8,128)(2,1)S(1)}, bf16[16,8,384]{2,1,0:T(8,128)(2,1)S(1)}, u32[]{:S(2)}, u32[]{:S(2)}) collective-permute-start(bf16[16,8,384]{2,1,0:T(8,128)(2,1)S(1)} %get-tuple-element.17), channel_id=1, source_target_pairs={{0,3},{1,0},{2,1},{3,2},{4,7},{5,4},{6,5},{7,6},{8,11},{9,8},{10,9... | collective-permute-start | bytes 294920 | tf_op jit(solution)/shard_map/side/ppermute | solution.py:278
  56.3 2.8 %collective-permute-start.1 = (bf16[16,8,384]{2,1,0:T(8,128)(2,1)S(1)}, bf16[16,8,384]{2,1,0:T(8,128)(2,1)S(1)}, u32[]{:S(2)}, u32[]{:S(2)}) collective-permute-start(bf16[16,8,384]{2,1,0:T(8,128)(2,1)S(1)} %get-tuple-element.18), channel_id=1, source_target_pairs={{0,2},{1,3},{2,0},{3,1},{4,6},{5,7},{6,4},{7,5},{8,10},{9,11},{10,... | collective-permute-start | bytes 294920 | tf_op jit(solution)/shard_map/side/ppermute | solution.py:278
  59.1 2.8 %collective-permute-start = (bf16[16,8,384]{2,1,0:T(8,128)(2,1)S(1)}, bf16[16,8,384]{2,1,0:T(8,128)(2,1)S(1)}, u32[]{:S(2)}, u32[]{:S(2)}) collective-permute-start(bf16[16,8,384]{2,1,0:T(8,128)(2,1)S(1)} %get-tuple-element.19), channel_id=1, source_target_pairs={{0,1},{1,2},{2,3},{3,0},{4,5},{5,6},{6,7},{7,4},{8,9},{9,10},{10,1... | collective-permute-start | bytes 294920 | tf_op jit(solution)/shard_map/side/ppermute | solution.py:278
  61.8 0.0 collective-permute-done.2.refs_3_
  61.8 4.3 %collective-permute-done.1.refs_2_ = bf16[16,8,384]{2,1,0:T(8,128)(2,1)S(1)} collective-permute-done((bf16[16,8,384]{2,1,0:T(8,128)(2,1)S(1)}, bf16[16,8,384]{2,1,0:T(8,128)(2,1)S(1)}, u32[]{:S(2)}, u32[]{:S(2)}) %collective-permute-start.1) | collective-permute-done | bytes 98336 | tf_op jit(solution)/shard_map/side/ppermute | solution.py:278
  66.2 1.3 %collective-permute-done.refs_1_ = bf16[16,8,384]{2,1,0:T(8,128)(2,1)S(1)} collective-permute-done((bf16[16,8,384]{2,1,0:T(8,128)(2,1)S(1)}, bf16[16,8,384]{2,1,0:T(8,128)(2,1)S(1)}, u32[]{:S(2)}, u32[]{:S(2)}) %collective-permute-start) | collective-permute-done | bytes 98336 | tf_op jit(solution)/shard_map/side/ppermute | solution.py:278
  67.5 0.0 copy-done.3
  67.5 0.0 copy-done.4
  67.5 1.0 early.1
  68.5 10.2 %all-to-all-done.1.green_ref = bf16[64,8,384]{2,1,0:T(8,128)(2,1)S(1)} async-done(((bf16[64,8,384]{2,1,0:T(8,128)(2,1)}), bf16[64,8,384]{2,1,0:T(8,128)(2,1)S(1)}, u32[]{:S(2)}, u32[]{:S(2)}) %all-to-all-start.1) | async-done | bytes 393248 | tf_op jit(solution)/shard_map/greens/all_to_all | solution.py:217
  78.7 2.9 %shard_map.68 = bf16[64,8,384]{2,1,0:T(8,128)(2,1)} custom-call(bf16[256,256]{1,0:T(8,128)(2,1)S(1)} %copy-done.4, bf16[256,256]{1,0:T(8,128)(2,1)S(1)} %copy-done.3, bf16[512,512]{1,0:T(8,128)(2,1)S(1)} %get-tuple-element.11.order_ref, bf16[512,512]{1,0:T(8,128)(2,1)S(1)} %get-tuple-element.12.back_ref, f32[4,256,192]{2,1,0:T(8,128)S(1)} %get-tuple-element.13.screen_ref, ...), custom_call_target="tpu_custom_call" | custom-call | tf_op jit(solution)/shard_map/pallas_call | solution.py:202
  81.6 5.5 %all-to-all-start.2 = ((bf16[64,8,384]{2,1,0:T(8,128)(2,1)}), bf16[64,8,384]{2,1,0:T(8,128)(2,1)S(1)}, u32[]{:S(2)}, u32[]{:S(2)}) async-start(bf16[64,8,384]{2,1,0:T(8,128)(2,1)} %shard_map.68), calls=%async_computation.2 | async-start | bytes 786432 | tf_op jit(solution)/shard_map/sigmas/all_to_all | solution.py:217
  87.1 0.1 copy.7.pattern_ref
  87.2 0.4 shard_map.64.select_ref
  87.6 26.5 %all-to-all-done.2.packed_ref = bf16[64,8,384]{2,1,0:T(8,128)(2,1)S(1)} async-done(((bf16[64,8,384]{2,1,0:T(8,128)(2,1)}), bf16[64,8,384]{2,1,0:T(8,128)(2,1)S(1)}, u32[]{:S(2)}, u32[]{:S(2)}) %all-to-all-start.2) | async-done | bytes 393248 | tf_op jit(solution)/shard_map/sigmas/all_to_all | solution.py:217
  114.1 1.3 %shard_map.69 = bf16[4,192,384]{2,1,0:T(8,128)(2,1)} custom-call(bf16[4,192,512]{2,1,0:T(8,128)(2,1)S(1)} %shard_map.64.select_ref, bf16[64,8,384]{2,1,0:T(8,128)(2,1)S(1)} %all-to-all-done.2.packed_ref), custom_call_target="tpu_custom_call" | custom-call | tf_op jit(solution)/shard_map/pallas_call | solution.py:202
  (1 shorter events, 0.0 us)
Async XLA Ops:
  2.7 15.4 %copy-start.2 = (bf16[2,2,192,384]{3,2,1,0:T(8,128)(2,1)S(1)}, bf16[2,2,192,384]{3,2,1,0:T(8,128)(2,1)}, u32[]{:S(2)}) copy-start(bf16[2,2,192,384]{3,2,1,0:T(8,128)(2,1)} %own_ref.1) | copy-start | bytes 1769476
  2.7 39.1 %all-to-all-start = ((bf16[16,32,384]{2,1,0:T(8,128)(2,1)}), bf16[16,32,384]{2,1,0:T(8,128)(2,1)S(1)}, u32[]{:S(2)}, u32[]{:S(2)}) async-start(bf16[16,32,384]{2,1,0:T(8,128)(2,1)} %shard_map.65), calls=%async_computation | async-start | bytes 786432 | tf_op jit(solution)/shard_map/screens/all_to_all | solution.py:217
  18.1 4.5 %collective-permute-start.3 = (bf16[2,2,192,384]{3,2,1,0:T(8,128)(2,1)S(1)}, bf16[2,2,192,384]{3,2,1,0:T(8,128)(2,1)S(1)}, u32[]{:S(2)}, u32[]{:S(2)}) collective-permute-start(bf16[2,2,192,384]{3,2,1,0:T(8,128)(2,1)S(1)} %copy-done.2), channel_id=1, source_target_pairs={{0,64},{128,192},{256,320},{384,448},{64,0},{192,128},{320,256},{4... | collective-permute-start | bytes 1769480 | tf_op jit(solution)/shard_map/halo/ppermute | solution.py:223
  20.0 11.2 %collective-permute-start.4 = (bf16[2,2,192,384]{3,2,1,0:T(8,128)(2,1)S(1)}, bf16[2,2,192,384]{3,2,1,0:T(8,128)(2,1)S(1)}, u32[]{:S(2)}, u32[]{:S(2)}) collective-permute-start(bf16[2,2,192,384]{3,2,1,0:T(8,128)(2,1)S(1)} %copy-done.2), channel_id=1, source_target_pairs={{64,128},{192,256},{320,384},{128,64},{256,192},{384,320},{65,129}... | collective-permute-start | bytes 1769480 | tf_op jit(solution)/shard_map/halo/ppermute | solution.py:223
  22.6 0.7 copy-start.5
  23.2 1.2 %copy-start = (bf16[2,3,192,384]{3,2,1,0:T(8,128)(2,1)S(1)}, bf16[2,3,192,384]{3,2,1,0:T(8,128)(2,1)}, u32[]{:S(2)}) copy-start(bf16[2,3,192,384]{3,2,1,0:T(8,128)(2,1)} %retarded_ref.3) | copy-start | bytes 2654212
  24.4 6.8 %copy-start.1 = (bf16[2,3,192,384]{3,2,1,0:T(8,128)(2,1)S(1)}, bf16[2,3,192,384]{3,2,1,0:T(8,128)(2,1)}, u32[]{:S(2)}) copy-start(bf16[2,3,192,384]{3,2,1,0:T(8,128)(2,1)} %retarded_ref.3) | copy-start | bytes 2654212
  41.9 36.9 %all-to-all-start.1 = ((bf16[64,8,384]{2,1,0:T(8,128)(2,1)}), bf16[64,8,384]{2,1,0:T(8,128)(2,1)S(1)}, u32[]{:S(2)}, u32[]{:S(2)}) async-start(bf16[64,8,384]{2,1,0:T(8,128)(2,1)} %shard_map.67), calls=%async_computation.1 | async-start | bytes 786432 | tf_op jit(solution)/shard_map/greens/all_to_all | solution.py:217
  51.4 16.1 %copy-start.3 = (bf16[256,256]{1,0:T(8,128)(2,1)S(1)}, bf16[256,256]{1,0:T(8,128)(2,1)}, u32[]{:S(2)}) copy-start(bf16[256,256]{1,0:T(8,128)(2,1)} %constant.18.clone.low_ref) | copy-start | bytes 393220
  51.4 16.1 %copy-start.4 = (bf16[256,256]{1,0:T(8,128)(2,1)S(1)}, bf16[256,256]{1,0:T(8,128)(2,1)}, u32[]{:S(2)}) copy-start(bf16[256,256]{1,0:T(8,128)(2,1)} %constant.17.clone.high_ref) | copy-start | bytes 393220
  51.5 10.4 %collective-permute-start.2 = (bf16[16,8,384]{2,1,0:T(8,128)(2,1)S(1)}, bf16[16,8,384]{2,1,0:T(8,128)(2,1)S(1)}, u32[]{:S(2)}, u32[]{:S(2)}) collective-permute-start(bf16[16,8,384]{2,1,0:T(8,128)(2,1)S(1)} %get-tuple-element.17), channel_id=1, source_target_pairs={{0,3},{1,0},{2,1},{3,2},{4,7},{5,4},{6,5},{7,6},{8,11},{9,8},{10,9... | collective-permute-start | bytes 294920 | tf_op jit(solution)/shard_map/side/ppermute | solution.py:278
  56.3 9.9 %collective-permute-start.1 = (bf16[16,8,384]{2,1,0:T(8,128)(2,1)S(1)}, bf16[16,8,384]{2,1,0:T(8,128)(2,1)S(1)}, u32[]{:S(2)}, u32[]{:S(2)}) collective-permute-start(bf16[16,8,384]{2,1,0:T(8,128)(2,1)S(1)} %get-tuple-element.18), channel_id=1, source_target_pairs={{0,2},{1,3},{2,0},{3,1},{4,6},{5,7},{6,4},{7,5},{8,10},{9,11},{10,... | collective-permute-start | bytes 294920 | tf_op jit(solution)/shard_map/side/ppermute | solution.py:278
  59.1 8.4 %collective-permute-start = (bf16[16,8,384]{2,1,0:T(8,128)(2,1)S(1)}, bf16[16,8,384]{2,1,0:T(8,128)(2,1)S(1)}, u32[]{:S(2)}, u32[]{:S(2)}) collective-permute-start(bf16[16,8,384]{2,1,0:T(8,128)(2,1)S(1)} %get-tuple-element.19), channel_id=1, source_target_pairs={{0,1},{1,2},{2,3},{3,0},{4,5},{5,6},{6,7},{7,4},{8,9},{9,10},{10,1... | collective-permute-start | bytes 294920 | tf_op jit(solution)/shard_map/side/ppermute | solution.py:278
  81.6 32.5 %all-to-all-start.2 = ((bf16[64,8,384]{2,1,0:T(8,128)(2,1)}), bf16[64,8,384]{2,1,0:T(8,128)(2,1)S(1)}, u32[]{:S(2)}, u32[]{:S(2)}) async-start(bf16[64,8,384]{2,1,0:T(8,128)(2,1)} %shard_map.68), calls=%async_computation.2 | async-start | bytes 786432 | tf_op jit(solution)/shard_map/sigmas/all_to_all | solution.py:217

commit v3 on v2

--- a/solution.py
+++ b/solution.py
@@ -14,6 +14,7 @@
 GROUPS = 64
 CHUNK = 8
 PACKED = GROUPS * CHUNK
+SCREEN_ROOT, GREEN_ROOT, SIGMA_ROOT = 0, 8, 8
 F32 = jnp.float32
 BF16 = jnp.bfloat16
 
@@ -52,7 +53,8 @@
         copy.start()
     place = iota((PACKED, 1), 0)
     chunk = place // CHUNK
-    wanted = (place % 2) * GROUPS + (chunk // 4) * 4 + (chunk + spot_ref[0]) % 4
+    device = (chunk // 4 + SCREEN_ROOT) % 16 * 4 + (chunk + spot_ref[0]) % 4
+    wanted = (place % 2) * GROUPS + device
     owner = (place % CHUNK) // 2
     copies[0].wait()
     rank = rank_row(pattern_ref[...])
@@ -81,7 +83,7 @@
     )
 
 
-def near_kernel(odd_ref, pattern_ref, retarded_ref, own_ref, near_ref, total_ref, live_ref, order_ref):
+def near_kernel(odd_ref, pattern_ref, retarded_ref, own_ref, near_ref, total_ref, live_ref):
     live = ones_where(rank_row(pattern_ref[...]) == iota((LIVE, 1), 0))
     live_ref[...] = live
     side = 2 - 2 * odd_ref[0]
@@ -89,9 +91,6 @@
         total = green_term(live, retarded_ref[energy, 1], own_ref, energy)
         total += green_term(live, retarded_ref[energy, side], near_ref, energy)
         total_ref[energy] = total
-    place = iota((PACKED, 1), 0)
-    source = (place % CHUNK) * GROUPS + place // CHUNK
-    order_ref[...] = ones_where(iota((PACKED, PACKED), 1) == source)
 
 
 def far_kernel(odd_ref, live_ref, retarded_ref, far_ref, total_ref, order_ref, out_ref):
@@ -111,47 +110,51 @@
     return real, imag
 
 
-def forward(high, low, real, imag, at):
+def transform(table_ref, cells):
+    out = jnp.dot(table_ref[...], cells, preferred_element_type=F32)
+    return out[: 2 * ENERGIES] + out[2 * ENERGIES :]
+
+
+def forward(table_ref, real, imag, at):
     rows = slice(at * ENERGIES, (at + 1) * ENERGIES)
-    stacked = jnp.concatenate([real[rows], imag[rows]], 0)
-    out = jnp.dot(high, stacked, preferred_element_type=F32)
-    return out + jnp.dot(low, stacked, preferred_element_type=F32)
-
-
-def screen_kernel(spot_ref, high_ref, low_ref, *refs):
+    return transform(table_ref, jnp.concatenate([real[rows], imag[rows]], 0))
+
+
+def screen_kernel(spot_ref, table_ref, *refs):
     screen_refs, (out_ref, order_ref, back_ref) = refs[:4], refs[4:]
     cell = iota((1, PACKED), 1)
     within = cell % ENERGIES
-    origin = (within // CHUNK) * 4 + (spot_ref[0] + 4 - cell // ENERGIES) % 4
+    origin = (within // CHUNK + SCREEN_ROOT) % 16 * 4 + (spot_ref[0] + 4 - cell // ENERGIES) % 4
     target = (cell % 4) * ENERGIES + origin * 2 + (cell % CHUNK) // 4
     order = ones_where(iota((PACKED, PACKED), 0) == target)
     cells = [ref[...].reshape(ENERGIES, 2 * B) for ref in screen_refs]
     real, imag = ordered(order, jnp.concatenate(cells, 0))
     for at in range(4):
-        out_ref[at] = forward(high_ref[...], low_ref[...], real, imag, at)
+        out_ref[at] = forward(table_ref, real, imag, at)
     place = iota((PACKED, 1), 0)
     energy = place % ENERGIES
-    source = (energy // 2) * CHUNK + (energy % 2) * 4 + place // ENERGIES
+    source = (energy // 2 + 64 - 4 * GREEN_ROOT) % GROUPS
+    source = source * CHUNK + (energy % 2) * 4 + place // ENERGIES
     order_ref[...] = ones_where(iota((PACKED, PACKED), 1) == source)
-    back = (place % 4) * ENERGIES + (place // CHUNK) * 2 + (place // 4) % 2
+    device = (place // CHUNK + 4 * SIGMA_ROOT) % GROUPS
+    back = (place % 4) * ENERGIES + device * 2 + (place // 4) % 2
     back_ref[...] = ones_where(iota((PACKED, PACKED), 1) == back)
 
 
-def convolve_kernel(high_ref, low_ref, order_ref, back_ref, screen_ref, green_ref, out_ref):
-    high, low = high_ref[...], low_ref[...]
+def convolve_kernel(table_ref, order_ref, back_ref, screen_ref, green_ref, out_ref):
     green = ordered(order_ref[...], green_ref[...].reshape(PACKED, 2 * B))
     factor = 1.0 / (ENERGIES * math.sqrt(ENERGIES))
     reals, imags = [], []
     for at in range(4):
-        out = forward(high, low, *green, at)
+        out = forward(table_ref, *green, at)
         gr, gi = out[:ENERGIES], out[ENERGIES:]
         wr, wi = screen_ref[at, :ENERGIES], screen_ref[at, ENERGIES:]
         prod = jnp.concatenate([gr * wr - gi * wi, -(gr * wi + gi * wr)], 0)
         prod_high = prod.astype(BF16)
         prod_low = (prod - prod_high.astype(F32)).astype(BF16)
-        out = jnp.dot(high, prod_high, preferred_element_type=F32)
+        high = table_ref[: 2 * ENERGIES]
+        out = transform(table_ref, prod_high)
         out += jnp.dot(high, prod_low, preferred_element_type=F32)
-        out += jnp.dot(low, prod_high, preferred_element_type=F32)
         out = (out * factor).astype(BF16)
         imags.append(out[:ENERGIES])
         reals.append(out[ENERGIES:])
@@ -164,18 +167,19 @@
 def select_kernel(pattern_ref, out_ref):
     rank = rank_column(pattern_ref[...])
     place = iota((1, PACKED), 1)
-    holds = (place % 2) * GROUPS + place // CHUNK
+    holds = (place % 2) * GROUPS + (place // CHUNK + 4 * SIGMA_ROOT) % GROUPS
     owner = (place % CHUNK) // 2
     for block in range(4):
-        out_ref[block] = ones_where(rank == jnp.where(owner == block, holds, -2))
+        rows = slice(block * B, (block + 1) * B)
+        out_ref[rows] = ones_where(rank == jnp.where(owner == block, holds, -2))
 
 
 def expand_kernel(select_ref, packed_ref, out_hbm, out_ref, sems):
     packed = packed_ref[...].reshape(PACKED, 2 * B)
+    rows = jnp.dot(select_ref[...], packed, preferred_element_type=F32)
     copies = []
     for block in range(4):
-        rows = jnp.dot(select_ref[block], packed, preferred_element_type=F32)
-        out_ref[block] = rows.astype(BF16)
+        out_ref[block] = rows[block * B : (block + 1) * B].astype(BF16)
         copies.append(
             pltpu.make_async_copy(out_ref.at[block], out_hbm.at[block], sems.at[block])
         )
@@ -191,7 +195,11 @@
     whole = np.block([[cosine, sine], [-sine, cosine]]).astype(np.float32)
     high = whole.astype(BF16)
     low = (whole - high.astype(np.float32)).astype(BF16)
-    return jnp.asarray(high), jnp.asarray(low)
+    place = np.arange(PACKED)
+    device = (place // CHUNK + 4 * GREEN_ROOT) % GROUPS
+    order = place % CHUNK * GROUPS + device
+    order = (np.arange(PACKED) == order[:, None]).astype(BF16)
+    return jnp.asarray(np.concatenate([high, low], 0)), jnp.asarray(order)
 
 
 VMEM, SMEM, HBM = pltpu.VMEM, pltpu.SMEM, pltpu.HBM
@@ -213,7 +221,11 @@
     return jax.ShapeDtypeStruct(shape, kind)
 
 
-def exchange(packed, groups=None):
+def along_z(root, side):
+    return [(root + z) % 16 * 4 + y for z in range(16) for y in side]
+
+
+def exchange(packed, groups):
     return lax.all_to_all(
         packed, "energy", split_axis=0, concat_axis=0, tiled=True, axis_index_groups=groups
     )
@@ -227,7 +239,7 @@
     packed = array((GROUPS, CHUNK, 2 * B))
     row, column = pattern.reshape(1, B), pattern.reshape(B, 1)
     spot = (lax.axis_index("energy") & 3).reshape(1)
-    high, low = tables()
+    table, interleave = tables()
     screen = call(
         pack_kernel,
         array((16, 4 * CHUNK, 2 * B)),
@@ -243,15 +255,15 @@
         ],
     )
     with jax.named_scope("screens"):
-        screen = exchange(screen, [[4 * z + y for z in range(16)] for y in range(4)])
+        screen = exchange(screen, [along_z(SCREEN_ROOT, (y,)) for y in range(4)])
     count = lax.axis_size("slab")
     odd = (lax.axis_index("slab") & 1).reshape(1)
     with jax.named_scope("halo"):
         far = swapped(injection, [(i, i + 1) for i in range(1, count - 1, 2)])
         near = swapped(injection, [(i, i + 1) for i in range(0, count, 2)])
-    total, live, order = call(
+    total, live = call(
         near_kernel,
-        [array((2, 2 * LIVE, 2 * B), F32), array((LIVE, B)), array((PACKED, PACKED))],
+        [array((2, 2 * LIVE, 2 * B), F32), array((LIVE, B))],
         odd,
         row,
         retarded,
@@ -267,11 +279,11 @@
         retarded,
         far,
         total,
-        order,
+        interleave,
         spaces=[SMEM] + [VMEM] * 5,
     )
     with jax.named_scope("greens"):
-        green = exchange(green)
+        green = exchange(green, [along_z(GREEN_ROOT, range(4))])
     screen = screen.reshape(16, 4, CHUNK, 2 * B)
     with jax.named_scope("side"):
         screen = [screen[:, 0]] + [
@@ -291,15 +303,14 @@
                 array((PACKED, PACKED)),
             ],
             spot,
-            high,
-            low,
+            table,
             *screen,
-            spaces=[SMEM] + [VMEM] * 6,
+            spaces=[SMEM] + [VMEM] * 5,
         )
-    sigma = call(convolve_kernel, packed, high, low, order, back, screen, green)
+    sigma = call(convolve_kernel, packed, table, order, back, screen, green)
     with jax.named_scope("sigmas"):
-        sigma = exchange(sigma)
-    select = call(select_kernel, array((4, B, PACKED)), column)
+        sigma = exchange(sigma, [along_z(SIGMA_ROOT, range(4))])
+    select = call(select_kernel, array((4 * B, PACKED)), column)
     out = call(
         expand_kernel,
         array((4, B, 2 * B)),

time: 116 us -> 111 us (0.957)
  waiting for transfers between devices: 55.5 us -> 34.7 us
  starting transfers between devices: 45.2 us -> 60.5 us
    all_to_all x3, waiting for transfers between devices: 45.3 us -> 24.8 us  [exchange(): lax.all_to_all(packed, 'energy', split_axis=0, concat_axis=0, tiled=True,...]
    all_to_all x3, starting transfers between devices: 30.3 us -> 45.8 us  [exchange(): lax.all_to_all(packed, 'energy', split_axis=0, concat_axis=0, tiled=True,...]
  transfers between devices with their start and end apart: 8 -> 8, of which waited for: 6 -> 5; matrix products, arithmetic and copies ran while one was open for 0% -> 0% of each run, Pallas kernels for 5% -> 5%
where the time goes in v3:
time: 111 us; the launch traced here: 110 us
  starting transfers between devices  60.5 us (55%)
  waiting for transfers between devices  34.7 us (31%)
  Pallas kernels  12.6 us (11%)
  local copies, waits for them, and re-layouts  2.01 us (2%)
    all_to_all x3, starting transfers between devices, exchange(): lax.all_to_all(packed, 'energy', split_axis=0, concat_axis=0, tiled=True,...  45.8 us
    all_to_all x3, waiting for transfers between devices, exchange(): lax.all_to_all(packed, 'energy', split_axis=0, concat_axis=0, tiled=True,...  24.8 us
    pallas_call x7, Pallas kernels, call(): pl.pallas_call(kernel, in_specs=[pl.BlockSpec(memory_space=space) for spa...  12.6 us
    ppermute x3, starting transfers between devices, local(): lax.ppermute(screen[:, step], 'energy', [(4 * z + y, 4 * z + (y + step) %...  10.3 us
    ppermute x3, waiting for transfers between devices, local(): lax.ppermute(screen[:, step], 'energy', [(4 * z + y, 4 * z + (y + step) %...  5.13 us
    ppermute x2, waiting for transfers between devices, swapped(): return lax.ppermute(cells, 'slab', pairs + [(b, a) for a, b in pairs])  4.76 us
    ppermute x2, starting transfers between devices, swapped(): return lax.ppermute(cells, 'slab', pairs + [(b, a) for a, b in pairs])  4.47 us
  transfers between devices with their start and end apart: 8, of which 5 were waited for; matrix products, arithmetic and copies ran while one was open for 0% of the time, Pallas kernels for 5%

profile of v3, /device:TPU:4, one launch (start us, length us, event | category | flops | bytes accessed | tf_op | source)
XLA Modules:
  0.0 110.0 jit_solution(17620442297059476995)
XLA Ops:
  0.0 2.7 %shard_map.65 = bf16[16,32,384]{2,1,0:T(8,128)(2,1)} custom-call(s32[1]{0:T(128)} %bitcast.1.spot_ref, s32[1,192]{1,0:T(1,128)} %bitcast.23, bf16[4,192,384]{2,1,0:T(8,128)(2,1)} %bitcast.27), custom_call_target="tpu_custom_call" | custom-call | tf_op jit(solution)/shard_map/pallas_call | solution.py:210
  2.7 0.0 copy-start.3
  2.7 15.3 %all-to-all-start = ((bf16[16,32,384]{2,1,0:T(8,128)(2,1)}), bf16[16,32,384]{2,1,0:T(8,128)(2,1)S(1)}, u32[]{:S(2)}, u32[]{:S(2)}) async-start(bf16[16,32,384]{2,1,0:T(8,128)(2,1)} %shard_map.65), calls=%async_computation | async-start | bytes 786432 | tf_op jit(solution)/shard_map/screens/all_to_all | solution.py:229
  18.1 0.0 copy-done.3
  18.1 1.9 %collective-permute-start.3 = (bf16[2,2,192,384]{3,2,1,0:T(8,128)(2,1)S(1)}, bf16[2,2,192,384]{3,2,1,0:T(8,128)(2,1)S(1)}, u32[]{:S(2)}, u32[]{:S(2)}) collective-permute-start(bf16[2,2,192,384]{3,2,1,0:T(8,128)(2,1)S(1)} %copy-done.3), channel_id=1, source_target_pairs={{0,64},{128,192},{256,320},{384,448},{64,0},{192,128},{320,256},{4... | collective-permute-start | bytes 1769480 | tf_op jit(solution)/shard_map/halo/ppermute | solution.py:235
  20.0 2.5 %collective-permute-start.4 = (bf16[2,2,192,384]{3,2,1,0:T(8,128)(2,1)S(1)}, bf16[2,2,192,384]{3,2,1,0:T(8,128)(2,1)S(1)}, u32[]{:S(2)}, u32[]{:S(2)}) collective-permute-start(bf16[2,2,192,384]{3,2,1,0:T(8,128)(2,1)S(1)} %copy-done.3), channel_id=1, source_target_pairs={{64,128},{192,256},{320,384},{128,64},{256,192},{384,320},{65,129}... | collective-permute-start | bytes 1769480 | tf_op jit(solution)/shard_map/halo/ppermute | solution.py:235
  22.6 0.0 copy-start.5
  22.6 0.0 collective-permute-done.3.near_ref
  22.6 0.7 copy-done.5
  23.2 0.0 copy-start
  23.2 1.2 %copy-done = bf16[2,3,192,384]{3,2,1,0:T(8,128)(2,1)S(1)} copy-done((bf16[2,3,192,384]{3,2,1,0:T(8,128)(2,1)S(1)}, bf16[2,3,192,384]{3,2,1,0:T(8,128)(2,1)}, u32[]{:S(2)}) %copy-start) | copy-done | bytes 884760
  24.4 0.0 copy-start.1
  24.4 0.0 copy-start.4
  24.4 2.0 %shard_map.66 = (f32[2,256,384]{2,1,0:T(8,128)S(1)}, bf16[128,192]{1,0:T(8,128)(2,1)S(1)}) custom-call(s32[1]{0:T(128)} %bitcast.9.odd_ref, s32[1,192]{1,0:T(1,128)S(1)} %bitcast.24, bf16[2,3,192,384]{3,2,1,0:T(8,128)(2,1)S(1)} %copy-done, bf16[2,2,192,384]{3,2,1,0:T(8,128)(2,1)S(1)} %copy-done.3, bf16[2,2,192,384]{3,2,1,0:T(8,128)(2,1)S(1)} %collective-permute-done.3.near_ref), custom_call_target="tpu_custom_call" | custom-call | tf_op jit(solution)/shard_map/pallas_call | solution.py:210
  26.4 4.8 %collective-permute-done.4.far_ref = bf16[2,2,192,384]{3,2,1,0:T(8,128)(2,1)S(1)} collective-permute-done((bf16[2,2,192,384]{3,2,1,0:T(8,128)(2,1)S(1)}, bf16[2,2,192,384]{3,2,1,0:T(8,128)(2,1)S(1)}, u32[]{:S(2)}, u32[]{:S(2)}) %collective-permute-start.4) | collective-permute-done | bytes 589856 | tf_op jit(solution)/shard_map/halo/ppermute | solution.py:235
  31.2 0.0 copy-done.1
  31.2 0.0 copy-done.4
  31.2 2.1 %shard_map.67 = bf16[64,8,384]{2,1,0:T(8,128)(2,1)} custom-call(s32[1]{0:T(128)} %bitcast.9.odd_ref, bf16[128,192]{1,0:T(8,128)(2,1)S(1)} %get-tuple-element.13.live_ref, bf16[2,3,192,384]{3,2,1,0:T(8,128)(2,1)S(1)} %copy-done.1, bf16[2,2,192,384]{3,2,1,0:T(8,128)(2,1)S(1)} %collective-permute-done.4.far_ref, ...), custom_call_target="tpu_custom_call" | custom-call | tf_op jit(solution)/shard_map/pallas_call | solution.py:210
  33.3 8.6 %all-to-all-done = bf16[16,32,384]{2,1,0:T(8,128)(2,1)S(1)} async-done(((bf16[16,32,384]{2,1,0:T(8,128)(2,1)}), bf16[16,32,384]{2,1,0:T(8,128)(2,1)S(1)}, u32[]{:S(2)}, u32[]{:S(2)}) %all-to-all-start) | async-done | bytes 393248 | tf_op jit(solution)/shard_map/screens/all_to_all | solution.py:229
  41.9 16.6 %all-to-all-start.1 = ((bf16[64,8,384]{2,1,0:T(8,128)(2,1)}), bf16[64,8,384]{2,1,0:T(8,128)(2,1)S(1)}, u32[]{:S(2)}, u32[]{:S(2)}) async-start(bf16[64,8,384]{2,1,0:T(8,128)(2,1)} %shard_map.67), calls=%async_computation.1 | async-start | bytes 786432 | tf_op jit(solution)/shard_map/greens/all_to_all | solution.py:229
  58.4 0.0 copy-start.2
  58.5 4.7 %collective-permute-start.2 = (bf16[16,8,384]{2,1,0:T(8,128)(2,1)S(1)}, bf16[16,8,384]{2,1,0:T(8,128)(2,1)S(1)}, u32[]{:S(2)}, u32[]{:S(2)}) collective-permute-start(bf16[16,8,384]{2,1,0:T(8,128)(2,1)S(1)} %get-tuple-element.15), channel_id=1, source_target_pairs={{0,3},{1,0},{2,1},{3,2},{4,7},{5,4},{6,5},{7,6},{8,11},{9,8},{10,9... | collective-permute-start | bytes 294920 | tf_op jit(solution)/shard_map/side/ppermute | solution.py:290
  63.2 2.8 %collective-permute-start.1 = (bf16[16,8,384]{2,1,0:T(8,128)(2,1)S(1)}, bf16[16,8,384]{2,1,0:T(8,128)(2,1)S(1)}, u32[]{:S(2)}, u32[]{:S(2)}) collective-permute-start(bf16[16,8,384]{2,1,0:T(8,128)(2,1)S(1)} %get-tuple-element.16), channel_id=1, source_target_pairs={{0,2},{1,3},{2,0},{3,1},{4,6},{5,7},{6,4},{7,5},{8,10},{9,11},{10,... | collective-permute-start | bytes 294920 | tf_op jit(solution)/shard_map/side/ppermute | solution.py:290
  66.0 2.8 %collective-permute-start = (bf16[16,8,384]{2,1,0:T(8,128)(2,1)S(1)}, bf16[16,8,384]{2,1,0:T(8,128)(2,1)S(1)}, u32[]{:S(2)}, u32[]{:S(2)}) collective-permute-start(bf16[16,8,384]{2,1,0:T(8,128)(2,1)S(1)} %get-tuple-element.17), channel_id=1, source_target_pairs={{0,1},{1,2},{2,3},{3,0},{4,5},{5,6},{6,7},{7,4},{8,9},{9,10},{10,1... | collective-permute-start | bytes 294920 | tf_op jit(solution)/shard_map/side/ppermute | solution.py:290
  68.8 0.0 collective-permute-done.2.refs_3_
  68.8 3.0 %collective-permute-done.1.refs_2_ = bf16[16,8,384]{2,1,0:T(8,128)(2,1)S(1)} collective-permute-done((bf16[16,8,384]{2,1,0:T(8,128)(2,1)S(1)}, bf16[16,8,384]{2,1,0:T(8,128)(2,1)S(1)}, u32[]{:S(2)}, u32[]{:S(2)}) %collective-permute-start.1) | collective-permute-done | bytes 98336 | tf_op jit(solution)/shard_map/side/ppermute | solution.py:290
  71.7 2.2 %collective-permute-done.refs_1_ = bf16[16,8,384]{2,1,0:T(8,128)(2,1)S(1)} collective-permute-done((bf16[16,8,384]{2,1,0:T(8,128)(2,1)S(1)}, bf16[16,8,384]{2,1,0:T(8,128)(2,1)S(1)}, u32[]{:S(2)}, u32[]{:S(2)}) %collective-permute-start) | collective-permute-done | bytes 98336 | tf_op jit(solution)/shard_map/side/ppermute | solution.py:290
  73.9 0.0 copy-done.2
  73.9 1.2 %early.1 = (f32[4,256,192]{2,1,0:T(8,128)S(1)}, bf16[512,512]{1,0:T(8,128)(2,1)S(1)}, bf16[512,512]{1,0:T(8,128)(2,1)S(1)}) custom-call(s32[1]{0:T(128)} %bitcast.1.spot_ref, bf16[512,256]{1,0:T(8,128)(2,1)S(1)} %copy-done.2, bf16[16,8,384]{2,1,0:T(8,128)(2,1)S(1)} %get-tuple-element.18.refs_0_, bf16[16,8,384]{2,1,0:T(8,128)(2,1)S(1)} %collective-permute-done.refs_1_, ...), custom_call_target="tpu_custom_call" | custom-call | tf_op jit(solution)/shard_map/early/pallas_call | solution.py:210
  75.1 0.0 all-to-all-done.1.green_ref
  75.2 2.9 %shard_map.68 = bf16[64,8,384]{2,1,0:T(8,128)(2,1)} custom-call(bf16[512,256]{1,0:T(8,128)(2,1)S(1)} %copy-done.2, bf16[512,512]{1,0:T(8,128)(2,1)S(1)} %get-tuple-element.10.order_ref, bf16[512,512]{1,0:T(8,128)(2,1)S(1)} %get-tuple-element.11.back_ref, f32[4,256,192]{2,1,0:T(8,128)S(1)} %get-tuple-element.12.screen_ref, ...), custom_call_target="tpu_custom_call" | custom-call | tf_op jit(solution)/shard_map/pallas_call | solution.py:210
  78.0 13.9 %all-to-all-start.2 = ((bf16[64,8,384]{2,1,0:T(8,128)(2,1)}), bf16[64,8,384]{2,1,0:T(8,128)(2,1)S(1)}, u32[]{:S(2)}, u32[]{:S(2)}) async-start(bf16[64,8,384]{2,1,0:T(8,128)(2,1)} %shard_map.68), calls=%async_computation.2 | async-start | bytes 786432 | tf_op jit(solution)/shard_map/sigmas/all_to_all | solution.py:229
  91.9 0.1 copy.7.pattern_ref
  92.0 0.4 shard_map.64.select_ref
  92.5 16.3 %all-to-all-done.2.packed_ref = bf16[64,8,384]{2,1,0:T(8,128)(2,1)S(1)} async-done(((bf16[64,8,384]{2,1,0:T(8,128)(2,1)}), bf16[64,8,384]{2,1,0:T(8,128)(2,1)S(1)}, u32[]{:S(2)}, u32[]{:S(2)}) %all-to-all-start.2) | async-done | bytes 393248 | tf_op jit(solution)/shard_map/sigmas/all_to_all | solution.py:229
  108.7 1.3 %shard_map.69 = bf16[4,192,384]{2,1,0:T(8,128)(2,1)} custom-call(bf16[768,512]{1,0:T(8,128)(2,1)S(1)} %shard_map.64.select_ref, bf16[64,8,384]{2,1,0:T(8,128)(2,1)S(1)} %all-to-all-done.2.packed_ref), custom_call_target="tpu_custom_call" | custom-call | tf_op jit(solution)/shard_map/pallas_call | solution.py:210
  (1 shorter events, 0.0 us)
Async XLA Ops:
  2.7 15.4 %copy-start.3 = (bf16[2,2,192,384]{3,2,1,0:T(8,128)(2,1)S(1)}, bf16[2,2,192,384]{3,2,1,0:T(8,128)(2,1)}, u32[]{:S(2)}) copy-start(bf16[2,2,192,384]{3,2,1,0:T(8,128)(2,1)} %own_ref.1) | copy-start | bytes 1769476
  2.7 39.1 %all-to-all-start = ((bf16[16,32,384]{2,1,0:T(8,128)(2,1)}), bf16[16,32,384]{2,1,0:T(8,128)(2,1)S(1)}, u32[]{:S(2)}, u32[]{:S(2)}) async-start(bf16[16,32,384]{2,1,0:T(8,128)(2,1)} %shard_map.65), calls=%async_computation | async-start | bytes 786432 | tf_op jit(solution)/shard_map/screens/all_to_all | solution.py:229
  18.1 4.5 %collective-permute-start.3 = (bf16[2,2,192,384]{3,2,1,0:T(8,128)(2,1)S(1)}, bf16[2,2,192,384]{3,2,1,0:T(8,128)(2,1)S(1)}, u32[]{:S(2)}, u32[]{:S(2)}) collective-permute-start(bf16[2,2,192,384]{3,2,1,0:T(8,128)(2,1)S(1)} %copy-done.3), channel_id=1, source_target_pairs={{0,64},{128,192},{256,320},{384,448},{64,0},{192,128},{320,256},{4... | collective-permute-start | bytes 1769480 | tf_op jit(solution)/shard_map/halo/ppermute | solution.py:235
  20.0 11.2 %collective-permute-start.4 = (bf16[2,2,192,384]{3,2,1,0:T(8,128)(2,1)S(1)}, bf16[2,2,192,384]{3,2,1,0:T(8,128)(2,1)S(1)}, u32[]{:S(2)}, u32[]{:S(2)}) collective-permute-start(bf16[2,2,192,384]{3,2,1,0:T(8,128)(2,1)S(1)} %copy-done.3), channel_id=1, source_target_pairs={{64,128},{192,256},{320,384},{128,64},{256,192},{384,320},{65,129}... | collective-permute-start | bytes 1769480 | tf_op jit(solution)/shard_map/halo/ppermute | solution.py:235
  22.6 0.7 copy-start.5
  23.2 1.2 %copy-start = (bf16[2,3,192,384]{3,2,1,0:T(8,128)(2,1)S(1)}, bf16[2,3,192,384]{3,2,1,0:T(8,128)(2,1)}, u32[]{:S(2)}) copy-start(bf16[2,3,192,384]{3,2,1,0:T(8,128)(2,1)} %retarded_ref.3) | copy-start | bytes 2654212
  24.4 6.8 %copy-start.1 = (bf16[2,3,192,384]{3,2,1,0:T(8,128)(2,1)S(1)}, bf16[2,3,192,384]{3,2,1,0:T(8,128)(2,1)}, u32[]{:S(2)}) copy-start(bf16[2,3,192,384]{3,2,1,0:T(8,128)(2,1)} %retarded_ref.3) | copy-start | bytes 2654212
  24.4 6.8 %copy-start.4 = (bf16[512,512]{1,0:T(8,128)(2,1)S(1)}, bf16[512,512]{1,0:T(8,128)(2,1)}, u32[]{:S(2)}) copy-start(bf16[512,512]{1,0:T(8,128)(2,1)} %constant.18.clone.order_ref) | copy-start | bytes 1572868
  41.9 33.3 %all-to-all-start.1 = ((bf16[64,8,384]{2,1,0:T(8,128)(2,1)}), bf16[64,8,384]{2,1,0:T(8,128)(2,1)S(1)}, u32[]{:S(2)}, u32[]{:S(2)}) async-start(bf16[64,8,384]{2,1,0:T(8,128)(2,1)} %shard_map.67), calls=%async_computation.1 | async-start | bytes 786432 | tf_op jit(solution)/shard_map/greens/all_to_all | solution.py:229
  58.4 15.5 %copy-start.2 = (bf16[512,256]{1,0:T(8,128)(2,1)S(1)}, bf16[512,256]{1,0:T(8,128)(2,1)}, u32[]{:S(2)}) copy-start(bf16[512,256]{1,0:T(8,128)(2,1)} %constant.17.clone.table_ref) | copy-start | bytes 786436
  58.5 10.3 %collective-permute-start.2 = (bf16[16,8,384]{2,1,0:T(8,128)(2,1)S(1)}, bf16[16,8,384]{2,1,0:T(8,128)(2,1)S(1)}, u32[]{:S(2)}, u32[]{:S(2)}) collective-permute-start(bf16[16,8,384]{2,1,0:T(8,128)(2,1)S(1)} %get-tuple-element.15), channel_id=1, source_target_pairs={{0,3},{1,0},{2,1},{3,2},{4,7},{5,4},{6,5},{7,6},{8,11},{9,8},{10,9... | collective-permute-start | bytes 294920 | tf_op jit(solution)/shard_map/side/ppermute | solution.py:290
  63.2 8.5 %collective-permute-start.1 = (bf16[16,8,384]{2,1,0:T(8,128)(2,1)S(1)}, bf16[16,8,384]{2,1,0:T(8,128)(2,1)S(1)}, u32[]{:S(2)}, u32[]{:S(2)}) collective-permute-start(bf16[16,8,384]{2,1,0:T(8,128)(2,1)S(1)} %get-tuple-element.16), channel_id=1, source_target_pairs={{0,2},{1,3},{2,0},{3,1},{4,6},{5,7},{6,4},{7,5},{8,10},{9,11},{10,... | collective-permute-start | bytes 294920 | tf_op jit(solution)/shard_map/side/ppermute | solution.py:290
  66.0 7.9 %collective-permute-start = (bf16[16,8,384]{2,1,0:T(8,128)(2,1)S(1)}, bf16[16,8,384]{2,1,0:T(8,128)(2,1)S(1)}, u32[]{:S(2)}, u32[]{:S(2)}) collective-permute-start(bf16[16,8,384]{2,1,0:T(8,128)(2,1)S(1)} %get-tuple-element.17), channel_id=1, source_target_pairs={{0,1},{1,2},{2,3},{3,0},{4,5},{5,6},{6,7},{7,4},{8,9},{9,10},{10,1... | collective-permute-start | bytes 294920 | tf_op jit(solution)/shard_map/side/ppermute | solution.py:290
  78.0 30.7 %all-to-all-start.2 = ((bf16[64,8,384]{2,1,0:T(8,128)(2,1)}), bf16[64,8,384]{2,1,0:T(8,128)(2,1)S(1)}, u32[]{:S(2)}, u32[]{:S(2)}) async-start(bf16[64,8,384]{2,1,0:T(8,128)(2,1)} %shard_map.68), calls=%async_computation.2 | async-start | bytes 786432 | tf_op jit(solution)/shard_map/sigmas/all_to_all | solution.py:229

commit v4 on v3

--- a/solution.py
+++ b/solution.py
@@ -14,13 +14,40 @@
 GROUPS = 64
 CHUNK = 8
 PACKED = GROUPS * CHUNK
-SCREEN_ROOT, GREEN_ROOT, SIGMA_ROOT = 0, 8, 8
+SCREEN_ORDER, GREEN_ORDER, SIGMA_ORDER = (12, False), (8, True), (8, True)
 F32 = jnp.float32
 BF16 = jnp.bfloat16
 
 
 def iota(shape, dim):
     return lax.broadcasted_iota(jnp.int32, shape, dim)
+
+
+def steps_at(slot):
+    odd, half = slot % 2, slot // 2
+    nonzero = (slot + 15) // 16
+    return nonzero * (8 + odd * half - (1 - odd) * half)
+
+
+def slot_of(steps):
+    late = steps // 8
+    nonzero = (steps + 15) // 16
+    return nonzero * (late * (2 * steps - 15) + (1 - late) * (16 - 2 * steps))
+
+
+def z_at(slot, order):
+    root, far_first = order
+    return (root + (steps_at(slot) if far_first else slot)) % 16
+
+
+def member(z, order):
+    root, far_first = order
+    steps = (z + 16 - root) % 16
+    return slot_of(steps) if far_first else steps
+
+
+def device_at(slot, order):
+    return z_at(slot // 4, order) * 4 + slot % 4
 
 
 def ones_where(condition):
@@ -53,7 +80,7 @@
         copy.start()
     place = iota((PACKED, 1), 0)
     chunk = place // CHUNK
-    device = (chunk // 4 + SCREEN_ROOT) % 16 * 4 + (chunk + spot_ref[0]) % 4
+    device = z_at(chunk // 4, SCREEN_ORDER) * 4 + (chunk + spot_ref[0]) % 4
     wanted = (place % 2) * GROUPS + device
     owner = (place % CHUNK) // 2
     copies[0].wait()
@@ -124,7 +151,7 @@
     screen_refs, (out_ref, order_ref, back_ref) = refs[:4], refs[4:]
     cell = iota((1, PACKED), 1)
     within = cell % ENERGIES
-    origin = (within // CHUNK + SCREEN_ROOT) % 16 * 4 + (spot_ref[0] + 4 - cell // ENERGIES) % 4
+    origin = z_at(within // CHUNK, SCREEN_ORDER) * 4 + (spot_ref[0] + 4 - cell // ENERGIES) % 4
     target = (cell % 4) * ENERGIES + origin * 2 + (cell % CHUNK) // 4
     order = ones_where(iota((PACKED, PACKED), 0) == target)
     cells = [ref[...].reshape(ENERGIES, 2 * B) for ref in screen_refs]
@@ -133,10 +160,10 @@
         out_ref[at] = forward(table_ref, real, imag, at)
     place = iota((PACKED, 1), 0)
     energy = place % ENERGIES
-    source = (energy // 2 + 64 - 4 * GREEN_ROOT) % GROUPS
+    source = member(energy // CHUNK, GREEN_ORDER) * 4 + energy // 2 % 4
     source = source * CHUNK + (energy % 2) * 4 + place // ENERGIES
     order_ref[...] = ones_where(iota((PACKED, PACKED), 1) == source)
-    device = (place // CHUNK + 4 * SIGMA_ROOT) % GROUPS
+    device = device_at(place // CHUNK, SIGMA_ORDER)
     back = (place % 4) * ENERGIES + device * 2 + (place // 4) % 2
     back_ref[...] = ones_where(iota((PACKED, PACKED), 1) == back)
 
@@ -167,7 +194,7 @@
 def select_kernel(pattern_ref, out_ref):
     rank = rank_column(pattern_ref[...])
     place = iota((1, PACKED), 1)
-    holds = (place % 2) * GROUPS + (place // CHUNK + 4 * SIGMA_ROOT) % GROUPS
+    holds = (place % 2) * GROUPS + device_at(place // CHUNK, SIGMA_ORDER)
     owner = (place % CHUNK) // 2
     for block in range(4):
         rows = slice(block * B, (block + 1) * B)
@@ -196,7 +223,7 @@
     high = whole.astype(BF16)
     low = (whole - high.astype(np.float32)).astype(BF16)
     place = np.arange(PACKED)
-    device = (place // CHUNK + 4 * GREEN_ROOT) % GROUPS
+    device = device_at(place // CHUNK, GREEN_ORDER)
     order = place % CHUNK * GROUPS + device
     order = (np.arange(PACKED) == order[:, None]).astype(BF16)
     return jnp.asarray(np.concatenate([high, low], 0)), jnp.asarray(order)
@@ -221,8 +248,8 @@
     return jax.ShapeDtypeStruct(shape, kind)
 
 
-def along_z(root, side):
-    return [(root + z) % 16 * 4 + y for z in range(16) for y in side]
+def along_z(order, side):
+    return [z_at(slot, order) * 4 + y for slot in range(16) for y in side]
 
 
 def exchange(packed, groups):
@@ -255,7 +282,7 @@
         ],
     )
     with jax.named_scope("screens"):
-        screen = exchange(screen, [along_z(SCREEN_ROOT, (y,)) for y in range(4)])
+        screen = exchange(screen, [along_z(SCREEN_ORDER, (y,)) for y in range(4)])
     count = lax.axis_size("slab")
     odd = (lax.axis_index("slab") & 1).reshape(1)
     with jax.named_scope("halo"):
@@ -283,7 +310,7 @@
         spaces=[SMEM] + [VMEM] * 5,
     )
     with jax.named_scope("greens"):
-        green = exchange(green, [along_z(GREEN_ROOT, range(4))])
+        green = exchange(green, [along_z(GREEN_ORDER, range(4))])
     screen = screen.reshape(16, 4, CHUNK, 2 * B)
     with jax.named_scope("side"):
         screen = [screen[:, 0]] + [
@@ -309,7 +336,7 @@
         )
     sigma = call(convolve_kernel, packed, table, order, back, screen, green)
     with jax.named_scope("sigmas"):
-        sigma = exchange(sigma, [along_z(SIGMA_ROOT, range(4))])
+        sigma = exchange(sigma, [along_z(SIGMA_ORDER, range(4))])
     select = call(select_kernel, array((4 * B, PACKED)), column)
     out = call(
         expand_kernel,

time: 111 us -> 109 us (0.982)
  waiting for transfers between devices: 34.7 us -> 33.4 us
    all_to_all x3, waiting for transfers between devices: 24.8 us -> 23.4 us  [exchange(): lax.all_to_all(packed, 'energy', split_axis=0, concat_axis=0, tiled=True,...]
  transfers between devices with their start and end apart: 8 -> 8, of which waited for: 5 -> 5; matrix products, arithmetic and copies ran while one was open for 0% -> 0% of each run, Pallas kernels for 5% -> 6%
where the time goes in v4:
time: 109 us; the launch traced here: 108 us
  starting transfers between devices  59.5 us (55%)
  waiting for transfers between devices  33.4 us (31%)
  Pallas kernels  13.4 us (12%)
  local copies, waits for them, and re-layouts  2.01 us (2%)
    all_to_all x3, starting transfers between devices, exchange(): lax.all_to_all(packed, 'energy', split_axis=0, concat_axis=0, tiled=True,...  44.8 us
    all_to_all x3, waiting for transfers between devices, exchange(): lax.all_to_all(packed, 'energy', split_axis=0, concat_axis=0, tiled=True,...  23.4 us
    pallas_call x7, Pallas kernels, call(): pl.pallas_call(kernel, in_specs=[pl.BlockSpec(memory_space=space) for spa...  13.4 us
    ppermute x3, starting transfers between devices, local(): lax.ppermute(screen[:, step], 'energy', [(4 * z + y, 4 * z + (y + step) %...  10.2 us
    ppermute x3, waiting for transfers between devices, local(): lax.ppermute(screen[:, step], 'energy', [(4 * z + y, 4 * z + (y + step) %...  5.23 us
    ppermute x2, waiting for transfers between devices, swapped(): return lax.ppermute(cells, 'slab', pairs + [(b, a) for a, b in pairs])  4.76 us
    ppermute x2, starting transfers between devices, swapped(): return lax.ppermute(cells, 'slab', pairs + [(b, a) for a, b in pairs])  4.47 us
  transfers between devices with their start and end apart: 8, of which 5 were waited for; matrix products, arithmetic and copies ran while one was open for 0% of the time, Pallas kernels for 6%

profile of v4, /device:TPU:4, one launch (start us, length us, event | category | flops | bytes accessed | tf_op | source)
XLA Modules:
  0.0 108.5 jit_solution(6788850484345107924)
XLA Ops:
  0.0 2.7 %shard_map.65 = bf16[16,32,384]{2,1,0:T(8,128)(2,1)} custom-call(s32[1]{0:T(128)} %bitcast.1.spot_ref, s32[1,192]{1,0:T(1,128)} %bitcast.23, bf16[4,192,384]{2,1,0:T(8,128)(2,1)} %bitcast.27), custom_call_target="tpu_custom_call" | custom-call | tf_op jit(solution)/shard_map/pallas_call | solution.py:237
  2.7 0.0 copy-start.3
  2.7 15.8 %all-to-all-start = ((bf16[16,32,384]{2,1,0:T(8,128)(2,1)}), bf16[16,32,384]{2,1,0:T(8,128)(2,1)S(1)}, u32[]{:S(2)}, u32[]{:S(2)}) async-start(bf16[16,32,384]{2,1,0:T(8,128)(2,1)} %shard_map.65), calls=%async_computation | async-start | bytes 786432 | tf_op jit(solution)/shard_map/screens/all_to_all | solution.py:256
  18.5 0.0 copy-done.3
  18.5 1.9 %collective-permute-start.3 = (bf16[2,2,192,384]{3,2,1,0:T(8,128)(2,1)S(1)}, bf16[2,2,192,384]{3,2,1,0:T(8,128)(2,1)S(1)}, u32[]{:S(2)}, u32[]{:S(2)}) collective-permute-start(bf16[2,2,192,384]{3,2,1,0:T(8,128)(2,1)S(1)} %copy-done.3), channel_id=1, source_target_pairs={{0,64},{128,192},{256,320},{384,448},{64,0},{192,128},{320,256},{4... | collective-permute-start | bytes 1769480 | tf_op jit(solution)/shard_map/halo/ppermute | solution.py:262
  20.5 2.5 %collective-permute-start.4 = (bf16[2,2,192,384]{3,2,1,0:T(8,128)(2,1)S(1)}, bf16[2,2,192,384]{3,2,1,0:T(8,128)(2,1)S(1)}, u32[]{:S(2)}, u32[]{:S(2)}) collective-permute-start(bf16[2,2,192,384]{3,2,1,0:T(8,128)(2,1)S(1)} %copy-done.3), channel_id=1, source_target_pairs={{64,128},{192,256},{320,384},{128,64},{256,192},{384,320},{65,129}... | collective-permute-start | bytes 1769480 | tf_op jit(solution)/shard_map/halo/ppermute | solution.py:262
  23.0 0.0 copy-start.5
  23.0 0.0 collective-permute-done.3.near_ref
  23.0 0.7 copy-done.5
  23.7 0.0 copy-start
  23.7 1.2 %copy-done = bf16[2,3,192,384]{3,2,1,0:T(8,128)(2,1)S(1)} copy-done((bf16[2,3,192,384]{3,2,1,0:T(8,128)(2,1)S(1)}, bf16[2,3,192,384]{3,2,1,0:T(8,128)(2,1)}, u32[]{:S(2)}) %copy-start) | copy-done | bytes 884760
  24.9 0.0 copy-start.1
  24.9 0.0 copy-start.4
  24.9 2.0 %shard_map.66 = (f32[2,256,384]{2,1,0:T(8,128)S(1)}, bf16[128,192]{1,0:T(8,128)(2,1)S(1)}) custom-call(s32[1]{0:T(128)} %bitcast.9.odd_ref, s32[1,192]{1,0:T(1,128)S(1)} %bitcast.24, bf16[2,3,192,384]{3,2,1,0:T(8,128)(2,1)S(1)} %copy-done, bf16[2,2,192,384]{3,2,1,0:T(8,128)(2,1)S(1)} %copy-done.3, bf16[2,2,192,384]{3,2,1,0:T(8,128)(2,1)S(1)} %collective-permute-done.3.near_ref), custom_call_target="tpu_custom_call" | custom-call | tf_op jit(solution)/shard_map/pallas_call | solution.py:237
  26.9 4.8 %collective-permute-done.4.far_ref = bf16[2,2,192,384]{3,2,1,0:T(8,128)(2,1)S(1)} collective-permute-done((bf16[2,2,192,384]{3,2,1,0:T(8,128)(2,1)S(1)}, bf16[2,2,192,384]{3,2,1,0:T(8,128)(2,1)S(1)}, u32[]{:S(2)}, u32[]{:S(2)}) %collective-permute-start.4) | collective-permute-done | bytes 589856 | tf_op jit(solution)/shard_map/halo/ppermute | solution.py:262
  31.7 0.0 copy-done.1
  31.7 0.0 copy-done.4
  31.7 2.1 %shard_map.67 = bf16[64,8,384]{2,1,0:T(8,128)(2,1)} custom-call(s32[1]{0:T(128)} %bitcast.9.odd_ref, bf16[128,192]{1,0:T(8,128)(2,1)S(1)} %get-tuple-element.13.live_ref, bf16[2,3,192,384]{3,2,1,0:T(8,128)(2,1)S(1)} %copy-done.1, bf16[2,2,192,384]{3,2,1,0:T(8,128)(2,1)S(1)} %collective-permute-done.4.far_ref, ...), custom_call_target="tpu_custom_call" | custom-call | tf_op jit(solution)/shard_map/pallas_call | solution.py:237
  33.8 6.6 %all-to-all-done = bf16[16,32,384]{2,1,0:T(8,128)(2,1)S(1)} async-done(((bf16[16,32,384]{2,1,0:T(8,128)(2,1)}), bf16[16,32,384]{2,1,0:T(8,128)(2,1)S(1)}, u32[]{:S(2)}, u32[]{:S(2)}) %all-to-all-start) | async-done | bytes 393248 | tf_op jit(solution)/shard_map/screens/all_to_all | solution.py:256
  40.4 15.2 %all-to-all-start.1 = ((bf16[64,8,384]{2,1,0:T(8,128)(2,1)}), bf16[64,8,384]{2,1,0:T(8,128)(2,1)S(1)}, u32[]{:S(2)}, u32[]{:S(2)}) async-start(bf16[64,8,384]{2,1,0:T(8,128)(2,1)} %shard_map.67), calls=%async_computation.1 | async-start | bytes 786432 | tf_op jit(solution)/shard_map/greens/all_to_all | solution.py:256
  55.6 0.0 copy-start.2
  55.6 4.7 %collective-permute-start.2 = (bf16[16,8,384]{2,1,0:T(8,128)(2,1)S(1)}, bf16[16,8,384]{2,1,0:T(8,128)(2,1)S(1)}, u32[]{:S(2)}, u32[]{:S(2)}) collective-permute-start(bf16[16,8,384]{2,1,0:T(8,128)(2,1)S(1)} %get-tuple-element.15), channel_id=1, source_target_pairs={{0,3},{1,0},{2,1},{3,2},{4,7},{5,4},{6,5},{7,6},{8,11},{9,8},{10,9... | collective-permute-start | bytes 294920 | tf_op jit(solution)/shard_map/side/ppermute | solution.py:317
  60.4 2.8 %collective-permute-start.1 = (bf16[16,8,384]{2,1,0:T(8,128)(2,1)S(1)}, bf16[16,8,384]{2,1,0:T(8,128)(2,1)S(1)}, u32[]{:S(2)}, u32[]{:S(2)}) collective-permute-start(bf16[16,8,384]{2,1,0:T(8,128)(2,1)S(1)} %get-tuple-element.16), channel_id=1, source_target_pairs={{0,2},{1,3},{2,0},{3,1},{4,6},{5,7},{6,4},{7,5},{8,10},{9,11},{10,... | collective-permute-start | bytes 294920 | tf_op jit(solution)/shard_map/side/ppermute | solution.py:317
  63.1 2.8 %collective-permute-start = (bf16[16,8,384]{2,1,0:T(8,128)(2,1)S(1)}, bf16[16,8,384]{2,1,0:T(8,128)(2,1)S(1)}, u32[]{:S(2)}, u32[]{:S(2)}) collective-permute-start(bf16[16,8,384]{2,1,0:T(8,128)(2,1)S(1)} %get-tuple-element.17), channel_id=1, source_target_pairs={{0,1},{1,2},{2,3},{3,0},{4,5},{5,6},{6,7},{7,4},{8,9},{9,10},{10,1... | collective-permute-start | bytes 294920 | tf_op jit(solution)/shard_map/side/ppermute | solution.py:317
  65.9 0.0 collective-permute-done.2.refs_3_
  65.9 2.9 %collective-permute-done.1.refs_2_ = bf16[16,8,384]{2,1,0:T(8,128)(2,1)S(1)} collective-permute-done((bf16[16,8,384]{2,1,0:T(8,128)(2,1)S(1)}, bf16[16,8,384]{2,1,0:T(8,128)(2,1)S(1)}, u32[]{:S(2)}, u32[]{:S(2)}) %collective-permute-start.1) | collective-permute-done | bytes 98336 | tf_op jit(solution)/shard_map/side/ppermute | solution.py:317
  68.8 2.3 %collective-permute-done.refs_1_ = bf16[16,8,384]{2,1,0:T(8,128)(2,1)S(1)} collective-permute-done((bf16[16,8,384]{2,1,0:T(8,128)(2,1)S(1)}, bf16[16,8,384]{2,1,0:T(8,128)(2,1)S(1)}, u32[]{:S(2)}, u32[]{:S(2)}) %collective-permute-start) | collective-permute-done | bytes 98336 | tf_op jit(solution)/shard_map/side/ppermute | solution.py:317
  71.1 0.0 copy-done.2
  71.1 2.0 %early.1 = (f32[4,256,192]{2,1,0:T(8,128)S(1)}, bf16[512,512]{1,0:T(8,128)(2,1)S(1)}, bf16[512,512]{1,0:T(8,128)(2,1)S(1)}) custom-call(s32[1]{0:T(128)} %bitcast.1.spot_ref, bf16[512,256]{1,0:T(8,128)(2,1)S(1)} %copy-done.2, bf16[16,8,384]{2,1,0:T(8,128)(2,1)S(1)} %get-tuple-element.18.refs_0_, bf16[16,8,384]{2,1,0:T(8,128)(2,1)S(1)} %collective-permute-done.refs_1_, ...), custom_call_target="tpu_custom_call" | custom-call | tf_op jit(solution)/shard_map/early/pallas_call | solution.py:237
  73.2 0.0 all-to-all-done.1.green_ref
  73.2 2.9 %shard_map.68 = bf16[64,8,384]{2,1,0:T(8,128)(2,1)} custom-call(bf16[512,256]{1,0:T(8,128)(2,1)S(1)} %copy-done.2, bf16[512,512]{1,0:T(8,128)(2,1)S(1)} %get-tuple-element.10.order_ref, bf16[512,512]{1,0:T(8,128)(2,1)S(1)} %get-tuple-element.11.back_ref, f32[4,256,192]{2,1,0:T(8,128)S(1)} %get-tuple-element.12.screen_ref, ...), custom_call_target="tpu_custom_call" | custom-call | tf_op jit(solution)/shard_map/pallas_call | solution.py:237
  76.1 13.8 %all-to-all-start.2 = ((bf16[64,8,384]{2,1,0:T(8,128)(2,1)}), bf16[64,8,384]{2,1,0:T(8,128)(2,1)S(1)}, u32[]{:S(2)}, u32[]{:S(2)}) async-start(bf16[64,8,384]{2,1,0:T(8,128)(2,1)} %shard_map.68), calls=%async_computation.2 | async-start | bytes 786432 | tf_op jit(solution)/shard_map/sigmas/all_to_all | solution.py:256
  89.9 0.1 copy.7.pattern_ref
  90.0 0.4 shard_map.64.select_ref
  90.4 16.8 %all-to-all-done.2.packed_ref = bf16[64,8,384]{2,1,0:T(8,128)(2,1)S(1)} async-done(((bf16[64,8,384]{2,1,0:T(8,128)(2,1)}), bf16[64,8,384]{2,1,0:T(8,128)(2,1)S(1)}, u32[]{:S(2)}, u32[]{:S(2)}) %all-to-all-start.2) | async-done | bytes 393248 | tf_op jit(solution)/shard_map/sigmas/all_to_all | solution.py:256
  107.2 1.3 %shard_map.69 = bf16[4,192,384]{2,1,0:T(8,128)(2,1)} custom-call(bf16[768,512]{1,0:T(8,128)(2,1)S(1)} %shard_map.64.select_ref, bf16[64,8,384]{2,1,0:T(8,128)(2,1)S(1)} %all-to-all-done.2.packed_ref), custom_call_target="tpu_custom_call" | custom-call | tf_op jit(solution)/shard_map/pallas_call | solution.py:237
  (1 shorter events, 0.0 us)
Async XLA Ops:
  2.7 15.8 %copy-start.3 = (bf16[2,2,192,384]{3,2,1,0:T(8,128)(2,1)S(1)}, bf16[2,2,192,384]{3,2,1,0:T(8,128)(2,1)}, u32[]{:S(2)}) copy-start(bf16[2,2,192,384]{3,2,1,0:T(8,128)(2,1)} %own_ref.1) | copy-start | bytes 1769476
  2.7 37.6 %all-to-all-start = ((bf16[16,32,384]{2,1,0:T(8,128)(2,1)}), bf16[16,32,384]{2,1,0:T(8,128)(2,1)S(1)}, u32[]{:S(2)}, u32[]{:S(2)}) async-start(bf16[16,32,384]{2,1,0:T(8,128)(2,1)} %shard_map.65), calls=%async_computation | async-start | bytes 786432 | tf_op jit(solution)/shard_map/screens/all_to_all | solution.py:256
  18.5 4.5 %collective-permute-start.3 = (bf16[2,2,192,384]{3,2,1,0:T(8,128)(2,1)S(1)}, bf16[2,2,192,384]{3,2,1,0:T(8,128)(2,1)S(1)}, u32[]{:S(2)}, u32[]{:S(2)}) collective-permute-start(bf16[2,2,192,384]{3,2,1,0:T(8,128)(2,1)S(1)} %copy-done.3), channel_id=1, source_target_pairs={{0,64},{128,192},{256,320},{384,448},{64,0},{192,128},{320,256},{4... | collective-permute-start | bytes 1769480 | tf_op jit(solution)/shard_map/halo/ppermute | solution.py:262
  20.5 11.2 %collective-permute-start.4 = (bf16[2,2,192,384]{3,2,1,0:T(8,128)(2,1)S(1)}, bf16[2,2,192,384]{3,2,1,0:T(8,128)(2,1)S(1)}, u32[]{:S(2)}, u32[]{:S(2)}) collective-permute-start(bf16[2,2,192,384]{3,2,1,0:T(8,128)(2,1)S(1)} %copy-done.3), channel_id=1, source_target_pairs={{64,128},{192,256},{320,384},{128,64},{256,192},{384,320},{65,129}... | collective-permute-start | bytes 1769480 | tf_op jit(solution)/shard_map/halo/ppermute | solution.py:262
  23.0 0.7 copy-start.5
  23.7 1.2 %copy-start = (bf16[2,3,192,384]{3,2,1,0:T(8,128)(2,1)S(1)}, bf16[2,3,192,384]{3,2,1,0:T(8,128)(2,1)}, u32[]{:S(2)}) copy-start(bf16[2,3,192,384]{3,2,1,0:T(8,128)(2,1)} %retarded_ref.3) | copy-start | bytes 2654212
  24.9 6.8 %copy-start.1 = (bf16[2,3,192,384]{3,2,1,0:T(8,128)(2,1)S(1)}, bf16[2,3,192,384]{3,2,1,0:T(8,128)(2,1)}, u32[]{:S(2)}) copy-start(bf16[2,3,192,384]{3,2,1,0:T(8,128)(2,1)} %retarded_ref.3) | copy-start | bytes 2654212
  24.9 6.8 %copy-start.4 = (bf16[512,512]{1,0:T(8,128)(2,1)S(1)}, bf16[512,512]{1,0:T(8,128)(2,1)}, u32[]{:S(2)}) copy-start(bf16[512,512]{1,0:T(8,128)(2,1)} %constant.18.clone.order_ref) | copy-start | bytes 1572868
  40.4 32.9 %all-to-all-start.1 = ((bf16[64,8,384]{2,1,0:T(8,128)(2,1)}), bf16[64,8,384]{2,1,0:T(8,128)(2,1)S(1)}, u32[]{:S(2)}, u32[]{:S(2)}) async-start(bf16[64,8,384]{2,1,0:T(8,128)(2,1)} %shard_map.67), calls=%async_computation.1 | async-start | bytes 786432 | tf_op jit(solution)/shard_map/greens/all_to_all | solution.py:256
  55.6 15.6 %copy-start.2 = (bf16[512,256]{1,0:T(8,128)(2,1)S(1)}, bf16[512,256]{1,0:T(8,128)(2,1)}, u32[]{:S(2)}) copy-start(bf16[512,256]{1,0:T(8,128)(2,1)} %constant.17.clone.table_ref) | copy-start | bytes 786436
  55.6 10.3 %collective-permute-start.2 = (bf16[16,8,384]{2,1,0:T(8,128)(2,1)S(1)}, bf16[16,8,384]{2,1,0:T(8,128)(2,1)S(1)}, u32[]{:S(2)}, u32[]{:S(2)}) collective-permute-start(bf16[16,8,384]{2,1,0:T(8,128)(2,1)S(1)} %get-tuple-element.15), channel_id=1, source_target_pairs={{0,3},{1,0},{2,1},{3,2},{4,7},{5,4},{6,5},{7,6},{8,11},{9,8},{10,9... | collective-permute-start | bytes 294920 | tf_op jit(solution)/shard_map/side/ppermute | solution.py:317
  60.4 8.5 %collective-permute-start.1 = (bf16[16,8,384]{2,1,0:T(8,128)(2,1)S(1)}, bf16[16,8,384]{2,1,0:T(8,128)(2,1)S(1)}, u32[]{:S(2)}, u32[]{:S(2)}) collective-permute-start(bf16[16,8,384]{2,1,0:T(8,128)(2,1)S(1)} %get-tuple-element.16), channel_id=1, source_target_pairs={{0,2},{1,3},{2,0},{3,1},{4,6},{5,7},{6,4},{7,5},{8,10},{9,11},{10,... | collective-permute-start | bytes 294920 | tf_op jit(solution)/shard_map/side/ppermute | solution.py:317
  63.1 8.0 %collective-permute-start = (bf16[16,8,384]{2,1,0:T(8,128)(2,1)S(1)}, bf16[16,8,384]{2,1,0:T(8,128)(2,1)S(1)}, u32[]{:S(2)}, u32[]{:S(2)}) collective-permute-start(bf16[16,8,384]{2,1,0:T(8,128)(2,1)S(1)} %get-tuple-element.17), channel_id=1, source_target_pairs={{0,1},{1,2},{2,3},{3,0},{4,5},{5,6},{6,7},{7,4},{8,9},{9,10},{10,1... | collective-permute-start | bytes 294920 | tf_op jit(solution)/shard_map/side/ppermute | solution.py:317
  76.1 31.1 %all-to-all-start.2 = ((bf16[64,8,384]{2,1,0:T(8,128)(2,1)}), bf16[64,8,384]{2,1,0:T(8,128)(2,1)S(1)}, u32[]{:S(2)}, u32[]{:S(2)}) async-start(bf16[64,8,384]{2,1,0:T(8,128)(2,1)} %shard_map.68), calls=%async_computation.2 | async-start | bytes 786432 | tf_op jit(solution)/shard_map/sigmas/all_to_all | solution.py:256

commit v5 on v4

--- a/solution.py
+++ b/solution.py
@@ -14,7 +14,7 @@
 GROUPS = 64
 CHUNK = 8
 PACKED = GROUPS * CHUNK
-SCREEN_ORDER, GREEN_ORDER, SIGMA_ORDER = (12, False), (8, True), (8, True)
+SCREEN_ORDER, GREEN_ORDER, SIGMA_ORDER = (12, False), (4, True), (4, True)
 F32 = jnp.float32
 BF16 = jnp.bfloat16
 

time: 109 us -> 110 us (level)
  waiting for transfers between devices: 33.4 us -> 40.1 us
  starting transfers between devices: 59.5 us -> 53.7 us
    all_to_all x3, waiting for transfers between devices: 23.4 us -> 30.1 us  [exchange(): lax.all_to_all(packed, 'energy', split_axis=0, concat_axis=0, tiled=True,...]
    all_to_all x3, starting transfers between devices: 44.8 us -> 39 us  [exchange(): lax.all_to_all(packed, 'energy', split_axis=0, concat_axis=0, tiled=True,...]
  transfers between devices with their start and end apart: 8 -> 8, of which waited for: 5 -> 6; matrix products, arithmetic and copies ran while one was open for 0% -> 0% of each run, Pallas kernels for 6% -> 6%
where the time goes in v5:
time: 110 us; the launch traced here: 109 us
  starting transfers between devices  53.7 us (49%)
  waiting for transfers between devices  40.1 us (36%)
  Pallas kernels  13.4 us (12%)
  local copies, waits for them, and re-layouts  2.01 us (2%)
    all_to_all x3, starting transfers between devices, exchange(): lax.all_to_all(packed, 'energy', split_axis=0, concat_axis=0, tiled=True,...  39 us
    all_to_all x3, waiting for transfers between devices, exchange(): lax.all_to_all(packed, 'energy', split_axis=0, concat_axis=0, tiled=True,...  30.1 us
    pallas_call x7, Pallas kernels, call(): pl.pallas_call(kernel, in_specs=[pl.BlockSpec(memory_space=space) for spa...  13.4 us
    ppermute x3, starting transfers between devices, local(): lax.ppermute(screen[:, step], 'energy', [(4 * z + y, 4 * z + (y + step) %...  10.3 us
    ppermute x3, waiting for transfers between devices, local(): lax.ppermute(screen[:, step], 'energy', [(4 * z + y, 4 * z + (y + step) %...  5.21 us
    ppermute x2, waiting for transfers between devices, swapped(): return lax.ppermute(cells, 'slab', pairs + [(b, a) for a, b in pairs])  4.76 us
    ppermute x2, starting transfers between devices, swapped(): return lax.ppermute(cells, 'slab', pairs + [(b, a) for a, b in pairs])  4.47 us
  transfers between devices with their start and end apart: 8, of which 6 were waited for; matrix products, arithmetic and copies ran while one was open for 0% of the time, Pallas kernels for 6%

profile of v5, /device:TPU:4, one launch (start us, length us, event | category | flops | bytes accessed | tf_op | source)
XLA Modules:
  0.0 109.3 jit_solution(309559156701445813)
XLA Ops:
  0.0 2.7 %shard_map.65 = bf16[16,32,384]{2,1,0:T(8,128)(2,1)} custom-call(s32[1]{0:T(128)} %bitcast.1.spot_ref, s32[1,192]{1,0:T(1,128)} %bitcast.23, bf16[4,192,384]{2,1,0:T(8,128)(2,1)} %bitcast.27), custom_call_target="tpu_custom_call" | custom-call | tf_op jit(solution)/shard_map/pallas_call | solution.py:237
  2.7 0.0 copy-start.3
  2.7 15.8 %all-to-all-start = ((bf16[16,32,384]{2,1,0:T(8,128)(2,1)}), bf16[16,32,384]{2,1,0:T(8,128)(2,1)S(1)}, u32[]{:S(2)}, u32[]{:S(2)}) async-start(bf16[16,32,384]{2,1,0:T(8,128)(2,1)} %shard_map.65), calls=%async_computation | async-start | bytes 786432 | tf_op jit(solution)/shard_map/screens/all_to_all | solution.py:256
  18.5 0.0 copy-done.3
  18.5 1.9 %collective-permute-start.3 = (bf16[2,2,192,384]{3,2,1,0:T(8,128)(2,1)S(1)}, bf16[2,2,192,384]{3,2,1,0:T(8,128)(2,1)S(1)}, u32[]{:S(2)}, u32[]{:S(2)}) collective-permute-start(bf16[2,2,192,384]{3,2,1,0:T(8,128)(2,1)S(1)} %copy-done.3), channel_id=1, source_target_pairs={{0,64},{128,192},{256,320},{384,448},{64,0},{192,128},{320,256},{4... | collective-permute-start | bytes 1769480 | tf_op jit(solution)/shard_map/halo/ppermute | solution.py:262
  20.5 2.5 %collective-permute-start.4 = (bf16[2,2,192,384]{3,2,1,0:T(8,128)(2,1)S(1)}, bf16[2,2,192,384]{3,2,1,0:T(8,128)(2,1)S(1)}, u32[]{:S(2)}, u32[]{:S(2)}) collective-permute-start(bf16[2,2,192,384]{3,2,1,0:T(8,128)(2,1)S(1)} %copy-done.3), channel_id=1, source_target_pairs={{64,128},{192,256},{320,384},{128,64},{256,192},{384,320},{65,129}... | collective-permute-start | bytes 1769480 | tf_op jit(solution)/shard_map/halo/ppermute | solution.py:262
  23.0 0.0 copy-start.5
  23.0 0.0 collective-permute-done.3.near_ref
  23.0 0.7 copy-done.5
  23.7 0.0 copy-start
  23.7 1.2 %copy-done = bf16[2,3,192,384]{3,2,1,0:T(8,128)(2,1)S(1)} copy-done((bf16[2,3,192,384]{3,2,1,0:T(8,128)(2,1)S(1)}, bf16[2,3,192,384]{3,2,1,0:T(8,128)(2,1)}, u32[]{:S(2)}) %copy-start) | copy-done | bytes 884760
  24.9 0.0 copy-start.1
  24.9 0.0 copy-start.4
  24.9 2.0 %shard_map.66 = (f32[2,256,384]{2,1,0:T(8,128)S(1)}, bf16[128,192]{1,0:T(8,128)(2,1)S(1)}) custom-call(s32[1]{0:T(128)} %bitcast.9.odd_ref, s32[1,192]{1,0:T(1,128)S(1)} %bitcast.24, bf16[2,3,192,384]{3,2,1,0:T(8,128)(2,1)S(1)} %copy-done, bf16[2,2,192,384]{3,2,1,0:T(8,128)(2,1)S(1)} %copy-done.3, bf16[2,2,192,384]{3,2,1,0:T(8,128)(2,1)S(1)} %collective-permute-done.3.near_ref), custom_call_target="tpu_custom_call" | custom-call | tf_op jit(solution)/shard_map/pallas_call | solution.py:237
  26.9 4.8 %collective-permute-done.4.far_ref = bf16[2,2,192,384]{3,2,1,0:T(8,128)(2,1)S(1)} collective-permute-done((bf16[2,2,192,384]{3,2,1,0:T(8,128)(2,1)S(1)}, bf16[2,2,192,384]{3,2,1,0:T(8,128)(2,1)S(1)}, u32[]{:S(2)}, u32[]{:S(2)}) %collective-permute-start.4) | collective-permute-done | bytes 589856 | tf_op jit(solution)/shard_map/halo/ppermute | solution.py:262
  31.7 0.0 copy-done.1
  31.7 0.0 copy-done.4
  31.7 2.1 %shard_map.67 = bf16[64,8,384]{2,1,0:T(8,128)(2,1)} custom-call(s32[1]{0:T(128)} %bitcast.9.odd_ref, bf16[128,192]{1,0:T(8,128)(2,1)S(1)} %get-tuple-element.13.live_ref, bf16[2,3,192,384]{3,2,1,0:T(8,128)(2,1)S(1)} %copy-done.1, bf16[2,2,192,384]{3,2,1,0:T(8,128)(2,1)S(1)} %collective-permute-done.4.far_ref, ...), custom_call_target="tpu_custom_call" | custom-call | tf_op jit(solution)/shard_map/pallas_call | solution.py:237
  33.8 6.6 %all-to-all-done = bf16[16,32,384]{2,1,0:T(8,128)(2,1)S(1)} async-done(((bf16[16,32,384]{2,1,0:T(8,128)(2,1)}), bf16[16,32,384]{2,1,0:T(8,128)(2,1)S(1)}, u32[]{:S(2)}, u32[]{:S(2)}) %all-to-all-start) | async-done | bytes 393248 | tf_op jit(solution)/shard_map/screens/all_to_all | solution.py:256
  40.4 13.3 %all-to-all-start.1 = ((bf16[64,8,384]{2,1,0:T(8,128)(2,1)}), bf16[64,8,384]{2,1,0:T(8,128)(2,1)S(1)}, u32[]{:S(2)}, u32[]{:S(2)}) async-start(bf16[64,8,384]{2,1,0:T(8,128)(2,1)} %shard_map.67), calls=%async_computation.1 | async-start | bytes 786432 | tf_op jit(solution)/shard_map/greens/all_to_all | solution.py:256
  53.6 0.0 copy-start.2
  53.7 4.7 %collective-permute-start.2 = (bf16[16,8,384]{2,1,0:T(8,128)(2,1)S(1)}, bf16[16,8,384]{2,1,0:T(8,128)(2,1)S(1)}, u32[]{:S(2)}, u32[]{:S(2)}) collective-permute-start(bf16[16,8,384]{2,1,0:T(8,128)(2,1)S(1)} %get-tuple-element.15), channel_id=1, source_target_pairs={{0,3},{1,0},{2,1},{3,2},{4,7},{5,4},{6,5},{7,6},{8,11},{9,8},{10,9... | collective-permute-start | bytes 294920 | tf_op jit(solution)/shard_map/side/ppermute | solution.py:317
  58.5 2.8 %collective-permute-start.1 = (bf16[16,8,384]{2,1,0:T(8,128)(2,1)S(1)}, bf16[16,8,384]{2,1,0:T(8,128)(2,1)S(1)}, u32[]{:S(2)}, u32[]{:S(2)}) collective-permute-start(bf16[16,8,384]{2,1,0:T(8,128)(2,1)S(1)} %get-tuple-element.16), channel_id=1, source_target_pairs={{0,2},{1,3},{2,0},{3,1},{4,6},{5,7},{6,4},{7,5},{8,10},{9,11},{10,... | collective-permute-start | bytes 294920 | tf_op jit(solution)/shard_map/side/ppermute | solution.py:317
  61.2 2.8 %collective-permute-start = (bf16[16,8,384]{2,1,0:T(8,128)(2,1)S(1)}, bf16[16,8,384]{2,1,0:T(8,128)(2,1)S(1)}, u32[]{:S(2)}, u32[]{:S(2)}) collective-permute-start(bf16[16,8,384]{2,1,0:T(8,128)(2,1)S(1)} %get-tuple-element.17), channel_id=1, source_target_pairs={{0,1},{1,2},{2,3},{3,0},{4,5},{5,6},{6,7},{7,4},{8,9},{9,10},{10,1... | collective-permute-start | bytes 294920 | tf_op jit(solution)/shard_map/side/ppermute | solution.py:317
  64.0 0.0 collective-permute-done.2.refs_3_
  64.0 2.9 %collective-permute-done.1.refs_2_ = bf16[16,8,384]{2,1,0:T(8,128)(2,1)S(1)} collective-permute-done((bf16[16,8,384]{2,1,0:T(8,128)(2,1)S(1)}, bf16[16,8,384]{2,1,0:T(8,128)(2,1)S(1)}, u32[]{:S(2)}, u32[]{:S(2)}) %collective-permute-start.1) | collective-permute-done | bytes 98336 | tf_op jit(solution)/shard_map/side/ppermute | solution.py:317
  66.9 2.3 %collective-permute-done.refs_1_ = bf16[16,8,384]{2,1,0:T(8,128)(2,1)S(1)} collective-permute-done((bf16[16,8,384]{2,1,0:T(8,128)(2,1)S(1)}, bf16[16,8,384]{2,1,0:T(8,128)(2,1)S(1)}, u32[]{:S(2)}, u32[]{:S(2)}) %collective-permute-start) | collective-permute-done | bytes 98336 | tf_op jit(solution)/shard_map/side/ppermute | solution.py:317
  69.2 0.0 copy-done.2
  69.2 2.0 %early.1 = (f32[4,256,192]{2,1,0:T(8,128)S(1)}, bf16[512,512]{1,0:T(8,128)(2,1)S(1)}, bf16[512,512]{1,0:T(8,128)(2,1)S(1)}) custom-call(s32[1]{0:T(128)} %bitcast.1.spot_ref, bf16[512,256]{1,0:T(8,128)(2,1)S(1)} %copy-done.2, bf16[16,8,384]{2,1,0:T(8,128)(2,1)S(1)} %get-tuple-element.18.refs_0_, bf16[16,8,384]{2,1,0:T(8,128)(2,1)S(1)} %collective-permute-done.refs_1_, ...), custom_call_target="tpu_custom_call" | custom-call | tf_op jit(solution)/shard_map/early/pallas_call | solution.py:237
  71.2 3.6 %all-to-all-done.1.green_ref = bf16[64,8,384]{2,1,0:T(8,128)(2,1)S(1)} async-done(((bf16[64,8,384]{2,1,0:T(8,128)(2,1)}), bf16[64,8,384]{2,1,0:T(8,128)(2,1)S(1)}, u32[]{:S(2)}, u32[]{:S(2)}) %all-to-all-start.1) | async-done | bytes 393248 | tf_op jit(solution)/shard_map/greens/all_to_all | solution.py:256
  74.8 2.9 %shard_map.68 = bf16[64,8,384]{2,1,0:T(8,128)(2,1)} custom-call(bf16[512,256]{1,0:T(8,128)(2,1)S(1)} %copy-done.2, bf16[512,512]{1,0:T(8,128)(2,1)S(1)} %get-tuple-element.10.order_ref, bf16[512,512]{1,0:T(8,128)(2,1)S(1)} %get-tuple-element.11.back_ref, f32[4,256,192]{2,1,0:T(8,128)S(1)} %get-tuple-element.12.screen_ref, ...), custom_call_target="tpu_custom_call" | custom-call | tf_op jit(solution)/shard_map/pallas_call | solution.py:237
  77.7 9.9 %all-to-all-start.2 = ((bf16[64,8,384]{2,1,0:T(8,128)(2,1)}), bf16[64,8,384]{2,1,0:T(8,128)(2,1)S(1)}, u32[]{:S(2)}, u32[]{:S(2)}) async-start(bf16[64,8,384]{2,1,0:T(8,128)(2,1)} %shard_map.68), calls=%async_computation.2 | async-start | bytes 786432 | tf_op jit(solution)/shard_map/sigmas/all_to_all | solution.py:256
  87.6 0.1 copy.7.pattern_ref
  87.7 0.4 shard_map.64.select_ref
  88.1 19.9 %all-to-all-done.2.packed_ref = bf16[64,8,384]{2,1,0:T(8,128)(2,1)S(1)} async-done(((bf16[64,8,384]{2,1,0:T(8,128)(2,1)}), bf16[64,8,384]{2,1,0:T(8,128)(2,1)S(1)}, u32[]{:S(2)}, u32[]{:S(2)}) %all-to-all-start.2) | async-done | bytes 393248 | tf_op jit(solution)/shard_map/sigmas/all_to_all | solution.py:256
  108.0 1.3 %shard_map.69 = bf16[4,192,384]{2,1,0:T(8,128)(2,1)} custom-call(bf16[768,512]{1,0:T(8,128)(2,1)S(1)} %shard_map.64.select_ref, bf16[64,8,384]{2,1,0:T(8,128)(2,1)S(1)} %all-to-all-done.2.packed_ref), custom_call_target="tpu_custom_call" | custom-call | tf_op jit(solution)/shard_map/pallas_call | solution.py:237
  (1 shorter events, 0.0 us)
Async XLA Ops:
  2.7 15.8 %copy-start.3 = (bf16[2,2,192,384]{3,2,1,0:T(8,128)(2,1)S(1)}, bf16[2,2,192,384]{3,2,1,0:T(8,128)(2,1)}, u32[]{:S(2)}) copy-start(bf16[2,2,192,384]{3,2,1,0:T(8,128)(2,1)} %own_ref.1) | copy-start | bytes 1769476
  2.7 37.6 %all-to-all-start = ((bf16[16,32,384]{2,1,0:T(8,128)(2,1)}), bf16[16,32,384]{2,1,0:T(8,128)(2,1)S(1)}, u32[]{:S(2)}, u32[]{:S(2)}) async-start(bf16[16,32,384]{2,1,0:T(8,128)(2,1)} %shard_map.65), calls=%async_computation | async-start | bytes 786432 | tf_op jit(solution)/shard_map/screens/all_to_all | solution.py:256
  18.5 4.5 %collective-permute-start.3 = (bf16[2,2,192,384]{3,2,1,0:T(8,128)(2,1)S(1)}, bf16[2,2,192,384]{3,2,1,0:T(8,128)(2,1)S(1)}, u32[]{:S(2)}, u32[]{:S(2)}) collective-permute-start(bf16[2,2,192,384]{3,2,1,0:T(8,128)(2,1)S(1)} %copy-done.3), channel_id=1, source_target_pairs={{0,64},{128,192},{256,320},{384,448},{64,0},{192,128},{320,256},{4... | collective-permute-start | bytes 1769480 | tf_op jit(solution)/shard_map/halo/ppermute | solution.py:262
  20.5 11.2 %collective-permute-start.4 = (bf16[2,2,192,384]{3,2,1,0:T(8,128)(2,1)S(1)}, bf16[2,2,192,384]{3,2,1,0:T(8,128)(2,1)S(1)}, u32[]{:S(2)}, u32[]{:S(2)}) collective-permute-start(bf16[2,2,192,384]{3,2,1,0:T(8,128)(2,1)S(1)} %copy-done.3), channel_id=1, source_target_pairs={{64,128},{192,256},{320,384},{128,64},{256,192},{384,320},{65,129}... | collective-permute-start | bytes 1769480 | tf_op jit(solution)/shard_map/halo/ppermute | solution.py:262
  23.0 0.7 copy-start.5
  23.7 1.2 %copy-start = (bf16[2,3,192,384]{3,2,1,0:T(8,128)(2,1)S(1)}, bf16[2,3,192,384]{3,2,1,0:T(8,128)(2,1)}, u32[]{:S(2)}) copy-start(bf16[2,3,192,384]{3,2,1,0:T(8,128)(2,1)} %retarded_ref.3) | copy-start | bytes 2654212
  24.9 6.8 %copy-start.1 = (bf16[2,3,192,384]{3,2,1,0:T(8,128)(2,1)S(1)}, bf16[2,3,192,384]{3,2,1,0:T(8,128)(2,1)}, u32[]{:S(2)}) copy-start(bf16[2,3,192,384]{3,2,1,0:T(8,128)(2,1)} %retarded_ref.3) | copy-start | bytes 2654212
  24.9 6.8 %copy-start.4 = (bf16[512,512]{1,0:T(8,128)(2,1)S(1)}, bf16[512,512]{1,0:T(8,128)(2,1)}, u32[]{:S(2)}) copy-start(bf16[512,512]{1,0:T(8,128)(2,1)} %constant.18.clone.order_ref) | copy-start | bytes 1572868
  40.4 34.5 %all-to-all-start.1 = ((bf16[64,8,384]{2,1,0:T(8,128)(2,1)}), bf16[64,8,384]{2,1,0:T(8,128)(2,1)S(1)}, u32[]{:S(2)}, u32[]{:S(2)}) async-start(bf16[64,8,384]{2,1,0:T(8,128)(2,1)} %shard_map.67), calls=%async_computation.1 | async-start | bytes 786432 | tf_op jit(solution)/shard_map/greens/all_to_all | solution.py:256
  53.6 15.6 %copy-start.2 = (bf16[512,256]{1,0:T(8,128)(2,1)S(1)}, bf16[512,256]{1,0:T(8,128)(2,1)}, u32[]{:S(2)}) copy-start(bf16[512,256]{1,0:T(8,128)(2,1)} %constant.17.clone.table_ref) | copy-start | bytes 786436
  53.7 10.3 %collective-permute-start.2 = (bf16[16,8,384]{2,1,0:T(8,128)(2,1)S(1)}, bf16[16,8,384]{2,1,0:T(8,128)(2,1)S(1)}, u32[]{:S(2)}, u32[]{:S(2)}) collective-permute-start(bf16[16,8,384]{2,1,0:T(8,128)(2,1)S(1)} %get-tuple-element.15), channel_id=1, source_target_pairs={{0,3},{1,0},{2,1},{3,2},{4,7},{5,4},{6,5},{7,6},{8,11},{9,8},{10,9... | collective-permute-start | bytes 294920 | tf_op jit(solution)/shard_map/side/ppermute | solution.py:317
  58.5 8.4 %collective-permute-start.1 = (bf16[16,8,384]{2,1,0:T(8,128)(2,1)S(1)}, bf16[16,8,384]{2,1,0:T(8,128)(2,1)S(1)}, u32[]{:S(2)}, u32[]{:S(2)}) collective-permute-start(bf16[16,8,384]{2,1,0:T(8,128)(2,1)S(1)} %get-tuple-element.16), channel_id=1, source_target_pairs={{0,2},{1,3},{2,0},{3,1},{4,6},{5,7},{6,4},{7,5},{8,10},{9,11},{10,... | collective-permute-start | bytes 294920 | tf_op jit(solution)/shard_map/side/ppermute | solution.py:317
  61.2 8.0 %collective-permute-start = (bf16[16,8,384]{2,1,0:T(8,128)(2,1)S(1)}, bf16[16,8,384]{2,1,0:T(8,128)(2,1)S(1)}, u32[]{:S(2)}, u32[]{:S(2)}) collective-permute-start(bf16[16,8,384]{2,1,0:T(8,128)(2,1)S(1)} %get-tuple-element.17), channel_id=1, source_target_pairs={{0,1},{1,2},{2,3},{3,0},{4,5},{5,6},{6,7},{7,4},{8,9},{9,10},{10,1... | collective-permute-start | bytes 294920 | tf_op jit(solution)/shard_map/side/ppermute | solution.py:317
  77.7 30.3 %all-to-all-start.2 = ((bf16[64,8,384]{2,1,0:T(8,128)(2,1)}), bf16[64,8,384]{2,1,0:T(8,128)(2,1)S(1)}, u32[]{:S(2)}, u32[]{:S(2)}) async-start(bf16[64,8,384]{2,1,0:T(8,128)(2,1)} %shard_map.68), calls=%async_computation.2 | async-start | bytes 786432 | tf_op jit(solution)/shard_map/sigmas/all_to_all | solution.py:256
